TPU v7x, 128 devices: a whole 4x4x4 slice. The times are simulated.
128 devices in a mesh: branch: 4 (over z_hi, core), seq: 8 (over z_lo, x), rep: 4 (over y).
Axes of the slice: x: 4, y: 4, z: 4 (z_hi: 2, z_lo: 2; z = z_hi * 2 + z_lo), core: 2. Of those that a mesh axis runs over, the one named last changes fastest.
Arguments:
- noisy: bfloat16 [4, 1024, 5120], P('rep'), may hold values from -6 to 6
- generated: bfloat16 [4, 1024, 5120], P('rep', 'seq'), may hold values from -170 to 170
- caption: bfloat16 [4, 5120], P('rep'), may hold values from -0.59765625 to 0.59765625
- null_caption: bfloat16 [5120], replicated, may hold values from -0.59765625 to 0.59765625
- caption_drop: int32 [4], P('rep'), may hold values from 0 to 1, as said below
- timestep: int32 [4], P('rep'), may hold values from 0 to 999
- window_start: int32 [4], P('rep'), may hold values from 0 to 31736
- teacher_qkv: bfloat16 [3, 5120, 4096], P(None, None, ('branch', 'seq')), may hold values from -0.078125 to 0.078125
- teacher_out: bfloat16 [4096, 5120], P(('branch', 'seq')), may hold values from -0.09375 to 0.09375
- teacher_gain: float32 [5120], replicated, may hold values from 0.5 to 1.5
- teacher_qk_gain: float32 [2, 4096], P(None, ('branch', 'seq')), may hold values from 0.7 to 2.6
- critic_qkv: bfloat16 [3, 5120, 4096], P(None, None, ('branch', 'seq')), may hold values from -0.078125 to 0.078125
- critic_out: bfloat16 [4096, 5120], P(('branch', 'seq')), may hold values from -0.09375 to 0.09375
- critic_gain: float32 [5120], replicated, may hold values from 0.5 to 1.5
- critic_qk_gain: float32 [2, 4096], P(None, ('branch', 'seq')), may hold values from 0.7 to 2.6
Outputs:
- generator_grad: bfloat16 [4, 1024, 5120], P('rep', 'seq')
- critic_qkv_grad: float32 [3, 5120, 4096], P(None, 'rep', ('branch', 'seq'))
- critic_out_grad: float32 [4096, 5120], P(('branch', 'seq'), 'rep')
Inputs may be any that keep to these rules, and one draw needn't show every extreme that they name: `caption_drop`: each window's flag is drawn independently.
All inputs are finite; a program needn't handle non-finite values. Where the computation divides by a largest or mean magnitude, that divisor is 1e-20 or more.
Results may differ from a plain program's by a relative error of at most 0.018.
The roundings to bfloat16 on the way count: a program that leaves them out, or rounds other values in their place, can miss the bound.
Values may be sent and summed in bfloat16 or wider, within the bound.
A program may use at most 192 MiB of HBM per device.

v0:
```python
import jax
import jax.numpy as jnp
from jax import lax
from jax.sharding import PartitionSpec as P

LEN = 1024
GRID_H = 30
GRID_W = 52


guidance = 5.0
score_scale = 128.0 ** (-0.5)
norm_eps = 1e-06


def rope_tables(first_token):
    token_index = first_token + jnp.arange(LEN, dtype=jnp.int32)
    plane_size = GRID_H * GRID_W
    frame_index = token_index // plane_size
    remainder = token_index - frame_index * plane_size
    row_index = remainder // GRID_W
    column_index = remainder - row_index * GRID_W
    pair_index = jnp.arange(64, dtype=jnp.int32)
    in_frames = pair_index < 22
    in_rows = jnp.logical_and(pair_index >= 22, pair_index < 43)
    local_rank = jnp.where(
        in_frames, pair_index, jnp.where(in_rows, pair_index - 22, pair_index - 43)
    ).astype(jnp.float32)
    axis_width = jnp.where(in_frames, 44.0, 42.0).astype(jnp.float32)
    frequency = jnp.exp(-jnp.log(10000.0) * 2.0 * local_rank / axis_width)
    chosen = jnp.where(
        in_frames[None, :],
        frame_index[:, None],
        jnp.where(in_rows[None, :], row_index[:, None], column_index[:, None]),
    ).astype(jnp.float32)
    angles = chosen * frequency[None, :]
    angles = jnp.concatenate([angles, angles], axis=1)
    return (jnp.cos(angles), jnp.sin(angles))


def rotate_half(values):
    return jnp.concatenate([-values[..., 64:], values[..., :64]], axis=-1)


def rotate_back(values):
    return jnp.concatenate([values[..., 64:], -values[..., :64]], axis=-1)


def norm_tokens(inputs, gain_values):
    scaled = (
        inputs
        * lax.rsqrt(jnp.mean(inputs * inputs, axis=-1, keepdims=True) + norm_eps)
        * gain_values
    )
    return scaled.astype(jnp.bfloat16)


def undo_norm(raw_values, inverse, gain_values, grad_normed):
    scaled = gain_values * grad_normed
    return inverse * scaled - raw_values * inverse * inverse * inverse * jnp.mean(
        scaled * raw_values, axis=-1, keepdims=True
    )


def head_forward(hidden, weights, qk_gains, cosine_table, sine_table):
    projected = jnp.einsum("bsd,kdc->kbsc", hidden, weights, preferred_element_type=jnp.float32)
    batch_size = hidden.shape[0]
    length = hidden.shape[1]
    query_raw = projected[0].reshape(batch_size, length, -1, 128)
    key_raw = projected[1].reshape(batch_size, length, -1, 128)
    value_rows = projected[2].reshape(batch_size, length, -1, 128).astype(jnp.bfloat16)
    gain_query = qk_gains[0].reshape(-1, 128)
    gain_key = qk_gains[1].reshape(-1, 128)
    inv_query = lax.rsqrt(jnp.mean(query_raw * query_raw, axis=-1, keepdims=True) + norm_eps)
    inv_key = lax.rsqrt(jnp.mean(key_raw * key_raw, axis=-1, keepdims=True) + norm_eps)
    normed_query = query_raw * inv_query * gain_query
    normed_key = key_raw * inv_key * gain_key
    cosine_h = cosine_table[:, :, None, :]
    sine_h = sine_table[:, :, None, :]
    rope_query = (normed_query * cosine_h + rotate_half(normed_query) * sine_h).astype(jnp.bfloat16)
    rope_key = (normed_key * cosine_h + rotate_half(normed_key) * sine_h).astype(jnp.bfloat16)
    scores = (
        jnp.einsum("bqhe,bkhe->bhqk", rope_query, rope_key, preferred_element_type=jnp.float32)
        * score_scale
    )
    exponent = jnp.exp(scores)
    probability = exponent / jnp.sum(exponent, axis=-1, keepdims=True)
    prob_rounded = probability.astype(jnp.bfloat16)
    attended = jnp.einsum(
        "bhqk,bkhe->bqhe", prob_rounded, value_rows, preferred_element_type=jnp.float32
    )
    attended = attended.astype(jnp.bfloat16).reshape(batch_size, length, -1)
    saved_state = (
        query_raw,
        key_raw,
        inv_query,
        inv_key,
        rope_query,
        rope_key,
        value_rows,
        probability,
        prob_rounded,
    )
    return (attended, saved_state)


def head_backward(hidden, grad_attn, saved_state, qk_gains, cosine_table, sine_table):
    (
        query_raw,
        key_raw,
        inv_query,
        inv_key,
        rope_query,
        rope_key,
        value_rows,
        probability,
        prob_rounded,
    ) = saved_state
    batch_size = hidden.shape[0]
    length = hidden.shape[1]
    grad_heads = grad_attn.reshape(batch_size, length, -1, 128)
    grad_prob = jnp.einsum(
        "bqhe,bkhe->bhqk", grad_heads, value_rows, preferred_element_type=jnp.float32
    )
    grad_score = (
        probability
        * (grad_prob - jnp.sum(grad_prob * probability, axis=-1, keepdims=True))
        * score_scale
    )
    grad_score = grad_score.astype(jnp.bfloat16)
    grad_qrot = jnp.einsum(
        "bhqk,bkhe->bqhe", grad_score, rope_key, preferred_element_type=jnp.float32
    )
    grad_krot = jnp.einsum(
        "bhqk,bqhe->bkhe", grad_score, rope_query, preferred_element_type=jnp.float32
    )
    grad_value = jnp.einsum(
        "bhqk,bqhe->bkhe", prob_rounded, grad_heads, preferred_element_type=jnp.float32
    )
    cosine_h = cosine_table[:, :, None, :]
    sine_h = sine_table[:, :, None, :]
    grad_qnorm = grad_qrot * cosine_h + rotate_back(grad_qrot * sine_h)
    grad_knorm = grad_krot * cosine_h + rotate_back(grad_krot * sine_h)
    grad_query = undo_norm(query_raw, inv_query, qk_gains[0].reshape(-1, 128), grad_qnorm)
    grad_key = undo_norm(key_raw, inv_key, qk_gains[1].reshape(-1, 128), grad_knorm)
    grad_stack = jnp.stack(
        [
            grad_query.reshape(batch_size, length, -1),
            grad_key.reshape(batch_size, length, -1),
            grad_value.reshape(batch_size, length, -1),
        ]
    ).astype(jnp.bfloat16)
    return jnp.einsum("bsd,kbsc->kdc", hidden, grad_stack, preferred_element_type=jnp.float32)


def body(
    noisy,
    generated,
    caption,
    null_caption,
    caption_drop,
    timestep,
    window_start,
    teacher_qkv,
    teacher_out,
    teacher_gain,
    teacher_qk_gain,
    critic_qkv,
    critic_out,
    critic_gain,
    critic_qk_gain,
):
    length = noisy.shape[1]
    width = noisy.shape[2]
    fraction = (timestep.astype(jnp.float32) + 1.0) / 1001.0
    noise_level = (5.0 * fraction / (1.0 + 4.0 * fraction))[:, None, None]
    used_caption = jnp.where(caption_drop[:, None] == 1, null_caption[None, :], caption)
    cond_shift = used_caption.astype(jnp.float32)[:, None, :]
    null_shift = null_caption.astype(jnp.float32)[None, None, :]
    latent = noisy.astype(jnp.float32)
    cond_normed = norm_tokens(latent + cond_shift, teacher_gain)
    null_normed = norm_tokens(latent + null_shift, teacher_gain)
    critic_normed = norm_tokens(latent + cond_shift, critic_gain)
    cosine_table, sine_table = jax.vmap(rope_tables)(window_start)
    cond_attn, unused = head_forward(
        cond_normed, teacher_qkv, teacher_qk_gain, cosine_table, sine_table
    )
    null_attn, unused = head_forward(
        null_normed, teacher_qkv, teacher_qk_gain, cosine_table, sine_table
    )
    fake_attn, saved_state = head_forward(
        critic_normed, critic_qkv, critic_qk_gain, cosine_table, sine_table
    )
    share_rows = length // lax.axis_size("seq")
    row_start = lax.axis_index("seq") * share_rows
    target = generated.astype(jnp.float32)
    fake_part = jnp.einsum("bsc,cd->sbd", fake_attn, critic_out, preferred_element_type=jnp.float32)
    cond_part = jnp.einsum(
        "bsc,cd->sbd", cond_attn, teacher_out, preferred_element_type=jnp.float32
    )
    null_part = jnp.einsum(
        "bsc,cd->sbd", null_attn, teacher_out, preferred_element_type=jnp.float32
    )
    seq_summed = lax.psum_scatter(
        jnp.stack([guidance * cond_part - (guidance - 1.0) * null_part, fake_part], axis=1).astype(
            jnp.bfloat16
        ),
        "seq",
        scatter_dimension=0,
        tiled=True,
    )
    summed = lax.psum(seq_summed, "branch").astype(jnp.float32)
    guided_rows = jnp.transpose(summed[:, 0], (1, 0, 2))
    fake_rows = jnp.transpose(summed[:, 1], (1, 0, 2))
    latent_rows = lax.dynamic_slice_in_dim(latent, row_start, share_rows, 1)
    cond_rows = latent_rows + cond_shift
    null_rows = latent_rows + null_shift
    real_velocity = guidance * cond_rows - (guidance - 1.0) * null_rows + guided_rows
    fake_velocity = cond_rows + fake_rows
    real_pred = latent_rows - noise_level * real_velocity
    fake_pred = latent_rows - noise_level * fake_velocity
    cotangent_rows = (-noise_level * (fake_pred - target) / 64.0).astype(jnp.bfloat16)
    slab_rows = lax.all_gather(cotangent_rows, "seq", axis=1, tiled=True)
    out_total = jnp.einsum("bsc,bsd->cd", fake_attn, slab_rows, preferred_element_type=jnp.float32)
    attn_slab = jnp.einsum("bsd,cd->bsc", slab_rows, critic_out, preferred_element_type=jnp.float32)
    grad_attn = attn_slab.astype(jnp.bfloat16)
    abs_total = lax.psum(jnp.sum(jnp.abs(real_pred - target), axis=(1, 2)), "seq")
    spread = abs_total / (length * width)
    generator_grad = ((fake_pred - real_pred) / (spread[:, None, None] + 1e-05)).astype(
        jnp.bfloat16
    )
    proj_share, out_share = (
        lax.psum_scatter(
            head_backward(
                critic_normed, grad_attn, saved_state, critic_qk_gain, cosine_table, sine_table
            ).astype(jnp.bfloat16),
            "rep",
            scatter_dimension=1,
            tiled=True,
        ).astype(jnp.float32),
        lax.psum_scatter(
            out_total.astype(jnp.bfloat16), "rep", scatter_dimension=1, tiled=True
        ).astype(jnp.float32),
    )
    return (generator_grad, proj_share, out_share)


def solution(mesh):
    in_specs = (
        P("rep", None, None),
        P("rep", "seq", None),
        P("rep", None),
        P(),
        P("rep"),
        P("rep"),
        P("rep"),
        P(None, None, ("branch", "seq")),
        P(("branch", "seq"), None),
        P(),
        P(None, ("branch", "seq")),
        P(None, None, ("branch", "seq")),
        P(("branch", "seq"), None),
        P(),
        P(None, ("branch", "seq")),
    )
    out_specs = (
        P("rep", "seq", None),
        P(None, "rep", ("branch", "seq")),
        P(("branch", "seq"), "rep"),
    )
    return jax.shard_map(body, mesh=mesh, in_specs=in_specs, out_specs=out_specs, check_vma=False)
```

profile of v0, /device:TPU:1, one launch (start us, length us, event | category | flops | bytes accessed | tf_op | source)
XLA Modules:
  0.0 632.6 jit_solution(15815109962702169643)
XLA Ops:
  8.7 6.3 copy.18
  15.1 9.9 %multiply_reduce_fusion = (f32[1024]{0:T(1024)S(1)}, f32[1024]{0:T(1024)S(1)}) fusion(bf16[1,1024,5120]{2,1,0:T(8,128)(2,1)} %param.15, f32[5120]{0:T(1024)S(1)} %convert_element_type.323, f32[5120]{0:T(1024)S(1)} %bitcast.413), kind=kLoop, calls=%fused_computation.4 | loop fusion | flops 36698112 | bytes 10534912 | tf_op jit(solution)/shard_map/reduce_sum | solution.py:52
  25.0 6.6 %fusion.1 = f32[1024,384]{0,1:S(1)} fusion(bf16[5120,384]{0,1:T(8,128)(2,1)} %bitcast.410, bf16[1,1024,5120]{2,1,0:T(8,128)(2,1)S(1)} %copy-done.3, f32[5120]{0:T(1024)S(1)} %copy-done.34, f32[1024]{0:T(1024)S(1)} %get-tuple-element.63, f32[5120]{0:T(1024)S(1)} %bitcast.414), kind=kOutput, calls=%fused_computation.8 | convolution fusion | flops 4052746240 | bytes 16035840
  31.8 4.4 fusion.4
  40.8 6.3 %copy.21 = bf16[3,5120,128]{1,2,0:T(8,128)(2,1)} copy(bf16[3,5120,128]{2,1,0:T(8,128)(2,1)} %param.26) | data formatting | bytes 7864320 | tf_op args[11]
  47.1 8.8 %fusion.12 = f32[1024,384]{0,1:S(1)} fusion(bf16[5120,384]{0,1:T(8,128)(2,1)} %bitcast.412, bf16[1,1024,5120]{2,1,0:T(8,128)(2,1)} %param.15, f32[5120]{0:T(1024)S(1)} %copy-done.35, f32[1024]{0:T(1024)S(1)} %get-tuple-element.63, f32[5120]{0:T(1024)S(1)} %bitcast.415), kind=kOutput, calls=%fused_computation.17 | convolution fusion | flops 4052746240 | bytes 16035840
  59.1 4.3 fusion.33
  66.7 5.9 convert_bitcast_fusion
  72.7 6.2 fusion.30
  78.9 11.7 %fusion.55 = f32[1024,5120]{1,0:T(8,128)} fusion(bf16[128,5120]{1,0:T(8,128)(2,1)S(1)} %copy-done, f32[1024,1024]{0,1:T(8,128)} %get-tuple-element.56, f32[1024]{0:T(1024)S(1)} %get-tuple-element.55, f32[3,1,1024,128]{2,3,0,1:T(8,128)} %bitcast.403), kind=kOutput, calls=%fused_computation.69 | convolution fusion | flops 1613889536 | bytes 26742784 | tf_op jit(solution)/shard_map/bsc,cd->sbd/dot_general | solution.py:198
  90.6 7.7 %fusion.31 = (f32[1024]{0:T(1024)S(1)}, f32[1024,1024]{0,1:T(8,128)}) fusion(f32[1024,1,1,1,1,64]{0,5,4,3,2,1:T(8,128)} %get-tuple-element.37, f32[1024,1,1,1,1,64]{0,5,4,3,2,1:T(8,128)} %get-tuple-element.36, f32[1024,1,1,1,1,64]{0,5,4,3,2,1:T(8,128)S(1)} %get-tuple-element.45, f32[1024]{0:T(1024)S(1)} %add_rsqrt_fusion.2, ...), kind=kOutput, calls=%fused_computation.38 | convolution fusion | flops 272628736 | bytes 6829056 | tf_op jit(solution)/shard_map/bqhe,bkhe->bhqk/dot_general | solution.py:83
  98.3 13.1 %fusion.20 = bf16[1024,1,1,5120]{3,0,2,1:T(8,128)(2,1)} fusion(bf16[128,5120]{1,0:T(8,128)(2,1)S(1)} %copy-done, f32[1024,5120]{1,0:T(8,128)} %fusion.55, f32[1024,1024]{0,1:T(8,128)} %get-tuple-element.58, f32[1024]{0:T(1024)S(1)} %get-tuple-element.57, f32[3,1,1024,128]{2,3,1,0:T(8,128)} %bitcast.409), kind=kOutput, calls=%fused_computation.26 | convolution fusion | flops 1634861056 | bytes 37228544 | tf_op jit(solution)/shard_map/bsc,cd->sbd/dot_general | solution.py:201
  111.4 17.2 %pad_maximum_fusion = bf16[1024,2,1,5120]{3,0,2,1:T(8,128)(2,1)} fusion(bf16[1024,1,1,5120]{3,0,2,1:T(8,128)(2,1)} %convert_bitcast_fusion, bf16[1024,1,1,5120]{3,0,2,1:T(8,128)(2,1)} %fusion.20), kind=kLoop, calls=%fused_computation | loop fusion | flops 10485760 | bytes 41943040 | tf_op jit(solution)/shard_map/stack | solution.py:205
  128.7 214.2 %reduce-scatter.4.cloned.1.call-done = bf16[128,2,1,5120]{3,0,2,1:T(8,128)(2,1)} async-done(((bf16[1024,2,1,5120]{3,0,2,1:T(8,128)(2,1)}), bf16[128,2,1,5120]{3,0,2,1:T(8,128)(2,1)}) %reduce-scatter.4.cloned.1.call-update) | async-done | bytes 2621456 | tf_op jit(solution)/shard_map/reduce_scatter | solution.py:204
  343.0 14.3 %convert_element_type.309 = f32[1,1024,5120]{2,1,0:T(8,128)} convert(bf16[1,1024,5120]{2,1,0:T(8,128)(2,1)} %param.15) | non-fusion elementwise | flops 5242880 | bytes 31457280 | tf_op jit(solution)/shard_map/convert_element_type | solution.py:180
  358.0 53.9 %all-reduce.2.cloned.1.call-done = bf16[128,2,1,5120]{3,0,2,1:T(8,128)(2,1)} async-done(((bf16[128,2,1,5120]{3,0,2,1:T(8,128)(2,1)}), bf16[128,2,1,5120]{3,0,2,1:T(8,128)(2,1)}) %all-reduce.2.cloned.1.call-update) | async-done | bytes 2621456 | tf_op jit(solution)/shard_map/psum | solution.py:212
  414.3 6.9 %fusion.38 = (bf16[1,128,5120]{2,1,0:T(8,128)(2,1)}, f32[]{:T(128)}) fusion(bf16[1,128,5120]{2,1,0:T(8,128)(2,1)S(1)} %copy-done.20, f32[]{:T(128)} %bitcast.97, f32[128,2,1,5120]{3,0,2,1:T(8,128)S(1)} %convert_element_type.344, f32[5120]{0:T(1024)S(1)} %bitcast.416, f32[]{:T(128)} %bitcast, f32[1,1024,5120]{2,1,0:T(8,128)} %convert_element_type.309, ...), kind=kLoop, calls=%fused_computation.47 | loop fusion | flops 12451839 | bytes 10526736 | tf_op jit(solution)/shard_map/convert_element_type | solution.py:222
  421.3 110.6 %all-gather.2.cloned.1.call-done = bf16[1,1024,5120]{2,1,0:T(8,128)(2,1)} async-done(((bf16[1,128,5120]{2,1,0:T(8,128)(2,1)}), bf16[1,1024,5120]{2,1,0:T(8,128)(2,1)}) %all-gather.2.cloned.1.call-update) | async-done | bytes 10485776 | tf_op jit(solution)/shard_map/all_gather | solution.py:223
  531.9 7.3 %fusion.49 = bf16[1024,128]{1,0:T(8,128)(2,1)S(1)} fusion(bf16[128,5120]{1,0:T(8,128)(2,1)} %param.27, bf16[1,1024,5120]{2,1,0:T(8,128)(2,1)} %all-gather.2.cloned.1.call-done), kind=kOutput, calls=%fused_computation.65 | convolution fusion | flops 1342308352 | bytes 12058624 | tf_op jit(solution)/shard_map/bsd,cd->bsc/dot_general | solution.py:225
  543.9 3.9 fusion.104
  561.6 6.3 fusion.24
  568.0 13.4 %psum.15 = f32[1]{0:T(128)} all-reduce(f32[1]{0:T(128)} %bitcast.92), channel_id=1, replica_groups=mesh['branch'=4,'seq'=8,'rep'=4] {'seq'}, use_global_device_ids=true, to_apply=%region_14.15 | all-reduce | flops 1 | bytes 8 | tf_op jit(solution)/shard_map/psum | solution.py:227
  582.1 5.6 divide_convert_fusion.2
  589.6 33.6 %reduce-scatter.6.cloned.1.call-done = bf16[3,1280,128]{1,2,0:T(8,128)(2,1)} async-done(((bf16[3,5120,128]{1,2,0:T(8,128)(2,1)}), bf16[3,1280,128]{1,2,0:T(8,128)(2,1)}) %reduce-scatter.6.cloned.1.call-update) | async-done | bytes 983056 | tf_op jit(solution)/shard_map/reduce_scatter | solution.py:233
  (142 shorter events, 36.3 us)
Async XLA Ops:
  7.2 71.7 %copy-start = (bf16[128,5120]{1,0:T(8,128)(2,1)S(1)}, bf16[128,5120]{1,0:T(8,128)(2,1)}, u32[]{:S(2)}) copy-start(bf16[128,5120]{1,0:T(8,128)(2,1)} %param.23) | copy-start | bytes 3932164
  7.2 7.9 %copy-start.30 = (bf16[5120]{0:T(1024)(128)(2,1)S(1)}, bf16[5120]{0:T(1024)(128)(2,1)}, u32[]{:S(2)}) copy-start(bf16[5120]{0:T(1024)(128)(2,1)} %param.18) | copy-start | bytes 30724
  7.2 7.9 %copy-start.31 = (bf16[1,5120]{1,0:T(2,128)(2,1)S(1)}, bf16[1,5120]{1,0:T(2,128)(2,1)}, u32[]{:S(2)}) copy-start(bf16[1,5120]{1,0:T(2,128)(2,1)} %param.17) | copy-start | bytes 30724
  7.2 335.7 %reduce-scatter.4.cloned.1.call-start = ((), (), s32[]{:S(2)}) async-start(), calls=%async_computation.3 | async-start | bytes 23592960 | tf_op jit(solution)/shard_map/reduce_scatter | solution.py:204
  15.1 9.9 %copy-start.3 = (bf16[1,1024,5120]{2,1,0:T(8,128)(2,1)S(1)}, bf16[1,1024,5120]{2,1,0:T(8,128)(2,1)}, u32[]{:S(2)}) copy-start(bf16[1,1024,5120]{2,1,0:T(8,128)(2,1)} %param.15) | copy-start | bytes 31457284
  15.1 9.9 %copy-start.34 = (f32[5120]{0:T(1024)S(1)}, f32[5120]{0:T(1024)}, u32[]{:S(2)}) copy-start(f32[5120]{0:T(1024)} %param.24) | copy-start | bytes 61444
  25.0 6.8 %copy-start.12 = (bf16[3,5120,128]{1,2,0:T(8,128)(2,1)S(1)}, bf16[3,5120,128]{1,2,0:T(8,128)(2,1)}, u32[]{:S(2)}) copy-start(bf16[3,5120,128]{1,2,0:T(8,128)(2,1)} %copy.18) | copy-start | bytes 11796484
  40.8 6.3 %copy-start.35 = (f32[5120]{0:T(1024)S(1)}, f32[5120]{0:T(1024)}, u32[]{:S(2)}) copy-start(f32[5120]{0:T(1024)} %param.28) | copy-start | bytes 61444
  47.1 9.0 %copy-start.33 = (f32[2,128]{1,0:T(2,128)S(1)}, f32[2,128]{1,0:T(2,128)}, u32[]{:S(2)}) copy-start(f32[2,128]{1,0:T(2,128)} %param.29) | copy-start | bytes 3076
  56.0 491.9 %copy-start.4 = (f32[1024,384]{0,1}, f32[1024,384]{0,1:S(1)}, u32[]{:S(2)}) copy-start(f32[1024,384]{0,1:S(1)} %fusion.12) | copy-start | bytes 4718596
  59.1 488.9 %copy-start.10 = (f32[1,1024,1,64]{1,3,2,0:T(8,128)}, f32[1,1024,1,64]{1,3,2,0:T(8,128)S(1)}, u32[]{:S(2)}) copy-start(f32[1,1024,1,64]{1,3,2,0:T(8,128)S(1)} %get-tuple-element.44) | copy-start | bytes 786436
  66.6 6.0 copy-start.26
  128.7 283.3 %all-reduce.2.cloned.1.call-start = ((), (), s32[]{:S(2)}) async-start(), calls=%async_computation.4 | async-start | bytes 5242880 | tf_op jit(solution)/shard_map/psum | solution.py:212
  342.9 188.9 %all-gather.2.cloned.1.call-start = ((), (), s32[]{:S(2)}) async-start(), calls=%async_computation.5 | async-start | bytes 11796480 | tf_op jit(solution)/shard_map/all_gather | solution.py:223
  357.2 57.1 %copy-start.20 = (bf16[1,128,5120]{2,1,0:T(8,128)(2,1)S(1)}, bf16[1,128,5120]{2,1,0:T(8,128)(2,1)}, u32[]{:S(2)}) copy-start(bf16[1,128,5120]{2,1,0:T(8,128)(2,1)} %param.16) | copy-start | bytes 3932164
  414.3 6.9 %copy-start.2 = (f32[128,2,1,5120]{3,0,2,1:T(8,128)}, f32[128,2,1,5120]{3,0,2,1:T(8,128)S(1)}, u32[]{:S(2)}) copy-start(f32[128,2,1,5120]{3,0,2,1:T(8,128)S(1)} %convert_element_type.344) | copy-start | bytes 15728644
  421.3 166.4 %reduce-scatter.8.cloned.1.call-start = ((), (), s32[]{:S(2)}) async-start(), calls=%async_computation.7 | async-start | bytes 1638400 | tf_op jit(solution)/shard_map/reduce_scatter | solution.py:241
  531.9 7.3 %copy-start.6 = (f32[1024,1024]{0,1:T(8,128)S(1)}, f32[1024,1024]{0,1:T(8,128)}, u32[]{:S(2)}) copy-start(f32[1024,1024]{0,1:T(8,128)} %copy-done.5) | copy-start | bytes 12582916
  540.3 10.1 %slice-start.3 = ((s8[10485760]{0:T(1024)(128)(4,1)}), s8[2097152]{0:T(1024)(128)(4,1)S(1)}, s32[]{:S(2)}) async-start(s8[10485760]{0:T(1024)(128)(4,1)} %bitcast.397), calls=%async_computation.11 | async-start | bytes 4194304
  540.3 10.1 %slice-start.4 = ((s8[10485760]{0:T(1024)(128)(4,1)}), s8[4194304]{0:T(1024)(128)(4,1)S(1)}, s32[]{:S(2)}) async-start(s8[10485760]{0:T(1024)(128)(4,1)} %bitcast.397), calls=%async_computation.12 | async-start | bytes 8388608
  543.9 6.6 %slice-start.5 = ((s8[10485760]{0:T(1024)(128)(4,1)}), s8[4194304]{0:T(1024)(128)(4,1)S(1)}, s32[]{:S(2)}) async-start(s8[10485760]{0:T(1024)(128)(4,1)} %bitcast.397), calls=%async_computation.13 | async-start | bytes 8388608
  553.1 6.9 %slice-start = ((s8[10485760]{0:T(1024)(128)(4,1)}), s8[2097152]{0:T(1024)(128)(4,1)S(1)}, s32[]{:S(2)}) async-start(s8[10485760]{0:T(1024)(128)(4,1)} %bitcast.386), calls=%async_computation.8 | async-start | bytes 4194304
  553.1 70.1 %reduce-scatter.6.cloned.1.call-start = ((), (), s32[]{:S(2)}) async-start(), calls=%async_computation.6 | async-start | bytes 4915200 | tf_op jit(solution)/shard_map/reduce_scatter | solution.py:233
  582.0 43.7 %copy-start.1 = (bf16[128,5120]{1,0:T(8,128)(2,1)S(1)}, bf16[128,5120]{1,0:T(8,128)(2,1)}, u32[]{:S(2)}) copy-start(bf16[128,5120]{1,0:T(8,128)(2,1)} %param.23) | copy-start | bytes 3932164
  (24 other events, 85.0 us)
Sparse Core Ops, SparseCore 0:
  128.8 214.0 reduce-scatter.3
  345.4 66.5 all-reduce.1
  421.4 110.4 all-gather.1
  553.2 21.9 reduce-scatter.7
  577.5 45.6 reduce-scatter.5
where the time goes:
time: 642 us; the launch traced here: 633 us
  waiting for transfers between devices  412 us (64%)
  matrix products  96.4 us (15%)
  other arithmetic  73.1 us (11%)
  local copies, waits for them, and re-layouts  19.4 us (3%)
  between operations  17.8 us (3%)
  blocking collectives  13.4 us (2%)
    reduce_scatter x1, waiting for transfers between devices, body(): lax.psum_scatter(jnp.stack([guidance * cond_part - (guidance - 1.0) * nul...  214 us
    all_gather x1, waiting for transfers between devices, body(): slab_rows = lax.all_gather(cotangent_rows, 'seq', axis=1, tiled=True)  111 us
    psum x1, waiting for transfers between devices, body(): summed = lax.psum(seq_summed, 'branch').astype(jnp.float32)  53.9 us
    reduce_scatter x1, waiting for transfers between devices, body(): lax.psum_scatter(head_backward(critic_normed, grad_attn, saved_state, cri...  33.6 us
    unnamed x3, matrix products  19.8 us
    unnamed x89, local copies, waits for them, and re-layouts  19.4 us
    dot_general x3, matrix products, head_forward(): jnp.einsum('bqhe,bkhe->bhqk', rope_query, rope_key, preferred_element_typ...  18.2 us
    another operation x1, other arithmetic, body(): jnp.stack([guidance * cond_part - (guidance - 1.0) * null_part, fake_part...  17.2 us
  transfers between devices with their start and end apart: 5, of which 4 were waited for; matrix products, arithmetic and copies ran while one was open for 6% of the time, Pallas kernels for 0%

commit v1 on v0

v1 whole, which is shorter than its diff:
```python
import jax
import jax.numpy as jnp
from jax import lax
from jax.experimental import pallas as pl
from jax.experimental.pallas import tpu as pltpu
from jax.sharding import PartitionSpec as P

LEN = 1024
GRID_H = 30
GRID_W = 52
D = 5120
HEAD = 128
NB = 32
ROWS = 256
COLS = 640
NR = LEN // ROWS
PAD = 16
BLK = ROWS + PAD
FEAT = 1280

guidance = 5.0
score_scale = 128.0 ** (-0.5)
norm_eps = 1e-06
f32 = jnp.float32
bf16 = jnp.bfloat16
MESH = pl.DeviceIdType.MESH


def rope_tables(first_token):
    token_index = first_token + jnp.arange(LEN, dtype=jnp.int32)
    plane_size = GRID_H * GRID_W
    frame_index = token_index // plane_size
    remainder = token_index - frame_index * plane_size
    row_index = remainder // GRID_W
    column_index = remainder - row_index * GRID_W
    pair_index = jnp.arange(64, dtype=jnp.int32)
    in_frames = pair_index < 22
    in_rows = jnp.logical_and(pair_index >= 22, pair_index < 43)
    local_rank = jnp.where(
        in_frames, pair_index, jnp.where(in_rows, pair_index - 22, pair_index - 43)
    ).astype(f32)
    axis_width = jnp.where(in_frames, 44.0, 42.0).astype(f32)
    frequency = jnp.exp(-jnp.log(10000.0) * 2.0 * local_rank / axis_width)
    chosen = jnp.where(
        in_frames[None, :],
        frame_index[:, None],
        jnp.where(in_rows[None, :], row_index[:, None], column_index[:, None]),
    ).astype(f32)
    angles = chosen * frequency[None, :]
    cosine = jnp.cos(angles)
    sine = jnp.sin(angles)
    return (
        jnp.concatenate([cosine, cosine], axis=1),
        jnp.concatenate([-sine, sine], axis=1),
    )


def dot(a, b):
    return jnp.dot(a, b, preferred_element_type=f32)


def dot_nt(a, b):
    return lax.dot_general(a, b, (((1,), (1,)), ((), ())), preferred_element_type=f32)


def dot_tn(a, b):
    return lax.dot_general(a, b, (((0,), (0,)), ((), ())), preferred_element_type=f32)


def half_turn(x):
    return pltpu.roll(x, 64, 1)


def step_kernel(
    noisy_h, wc_h, wt_h, caps_h, cos_h, sin_h, cqk, tqk, level, caps, cgain, gen_h, cout_h, tout_h,
    gg_h, qg_h, og_h, ogin_h,
    noisy, wcx, wtx, ac, ag, gain_in, qgin, og8in, diff_in, abs_in, gen, cos, sin,
    qraw, kraw, qr, kr, vv, rc, rn, invq, invk, linv, fa, gt,
    lsem, rsem, ssem,
):
    b = lax.axis_index("branch")
    s = lax.axis_index("seq")
    w = lax.axis_index("rep")
    me = b * 8 + s
    myc = b * 2 + lax.rem(s, 2)
    myr = s // 2

    def plane(q):
        return {"branch": q // 8, "seq": lax.rem(q, 8)}

    def col_of(q):
        return (q // 8) * 2 + lax.rem(q, 2)

    def row_of(q):
        return lax.rem(q, 8) // 2

    def peer(k):
        return lax.rem(me + k, NB)

    EW, EG, ET, EA, EU, EB, EO, ED, ES, EQ, E8 = range(11)

    def send(src, dst, e, device):
        pltpu.make_async_remote_copy(
            src_ref=src, dst_ref=dst, send_sem=ssem.at[e], recv_sem=rsem.at[e],
            device_id=device, device_id_type=MESH,
        ).start()

    def local(src, dst, sem):
        c = pltpu.make_async_copy(src, dst, sem)
        c.start()
        return c

    def wait_bytes(ref, sem):
        pltpu.make_async_copy(ref, ref, sem).wait()

    for i in range(NR):
        local(noisy_h.at[pl.ds(i * ROWS, ROWS), :], noisy.at[i, pl.ds(0, ROWS), :], lsem.at[i])
    cap_copies = [local(caps_h, noisy.at[i, pl.ds(ROWS, PAD), :], lsem.at[4 + i]) for i in range(NR)]
    cos_copy = local(cos_h, cos, lsem.at[8])
    sin_copy = local(sin_h, sin, lsem.at[9])

    barrier = pltpu.get_barrier_semaphore()

    @pl.loop(1, NB)
    def _(k):
        pl.semaphore_signal(barrier, inc=1, device_id=plane(peer(k)), device_id_type=MESH)

    for k in range(1, 4):
        pl.semaphore_signal(
            barrier, inc=1, device_id={"rep": lax.rem(w + k, 4)}, device_id_type=MESH
        )
    pl.semaphore_wait(barrier, NB - 1 + 3)

    def weights(src, dst, e):
        mine = dst.at[pl.ds(me * HEAD, HEAD), :]

        @pl.loop(1, NB)
        def _(k):
            q = peer(k)
            send(src.at[:, pl.ds(pl.multiple_of(col_of(q) * COLS, COLS), COLS)], mine, e, plane(q))

        local(src.at[:, pl.ds(pl.multiple_of(myc * COLS, COLS), COLS)], mine, rsem.at[e])

    weights(cout_h, wcx, EW)
    partner = me + 1 - 2 * lax.rem(s, 2)
    gen_rows = gen.at[pl.ds(pl.multiple_of(lax.rem(s, 2) * 128, 128), 128), :]
    send(
        gen_h.at[:, pl.ds(pl.multiple_of(col_of(partner) * COLS, COLS), COLS)],
        gen_rows, EG, plane(partner),
    )
    local(gen_h.at[:, pl.ds(pl.multiple_of(myc * COLS, COLS), COLS)], gen_rows, rsem.at[EG])

    def tokens(src, dst, e):
        mine = dst.at[:, pl.ds(pl.multiple_of(me * HEAD, HEAD), HEAD)]

        @pl.loop(1, NB)
        def _(k):
            q = peer(k)
            send(src.at[pl.ds(pl.multiple_of(row_of(q) * ROWS, ROWS), ROWS), :], mine, e, plane(q))

        local(src.at[pl.ds(pl.multiple_of(myr * ROWS, ROWS), ROWS), :], mine, rsem.at[e])

    def forward_phase(wall, pbuf, att_a):
        def load_w(j):
            src = wc_h if j < 3 else wt_h
            return local(src.at[j % 3], wall.at[:, pl.ds(j * HEAD, HEAD)], lsem.at[10 + j])

        w_copies = [load_w(j) for j in range(6)]

        for c in cap_copies:
            c.wait()
        for c in w_copies[:4]:
            c.wait()

        @pl.loop(0, NR)
        def _(i):
            pltpu.make_async_copy(
                noisy_h.at[pl.ds(i * ROWS, ROWS), :], noisy.at[i, pl.ds(0, ROWS), :], lsem.at[i]
            ).wait()
            pbuf[i, :, 0:512] = dot(noisy[i], wall[:, 0:512])
            for half in range(2):
                top = half * 128
                acc_c = jnp.zeros((128, 128), f32)
                acc_n = jnp.zeros((128, 128), f32)
                for j in range(D // 128):
                    x = noisy[i, top : top + 128, j * 128 : j * 128 + 128].astype(f32)
                    u = x + caps[0:1, j * 128 : j * 128 + 128]
                    v = x + caps[1:2, j * 128 : j * 128 + 128]
                    acc_c += u * u
                    acc_n += v * v
                sum_c = jnp.sum(acc_c, axis=1, keepdims=True) * (1.0 / D)
                sum_n = jnp.sum(acc_n, axis=1, keepdims=True) * (1.0 / D)
                rc[i, top : top + 128, :] = jnp.broadcast_to(
                    lax.rsqrt(sum_c + norm_eps), (128, 128)
                )
                rn[i, top : top + 128, :] = jnp.broadcast_to(
                    lax.rsqrt(sum_n + norm_eps), (128, 128)
                )

        cos_copy.wait()
        sin_copy.wait()

        def attention(col, row, scale_ref, gains, keep, out):
            @pl.loop(0, NR)
            def _(i):
                rows = pl.ds(pl.multiple_of(i * ROWS, ROWS), ROWS)
                scale = scale_ref[i]
                cosine = cos[rows, :]
                sine = sin[rows, :]

                def raw(m):
                    block = pbuf[i, 0:ROWS, col + m * HEAD : col + (m + 1) * HEAD]
                    shift = pbuf[
                        i, ROWS + row : ROWS + row + 1, col + m * HEAD : col + (m + 1) * HEAD
                    ]
                    return scale * (block + shift)

                for m, (dst, raw_ref, inv_ref) in enumerate(((qr, qraw, invq), (kr, kraw, invk))):
                    x = raw(m)
                    inverse = lax.rsqrt(jnp.mean(x * x, axis=1, keepdims=True) + norm_eps)
                    normed = x * inverse * gains[m : m + 1, :]
                    dst[rows, :] = (normed * cosine + half_turn(normed) * sine).astype(bf16)
                    if keep:
                        raw_ref[rows, :] = x
                        inv_ref[rows, :] = jnp.broadcast_to(inverse, (ROWS, HEAD))
                vv[rows, :] = raw(2).astype(bf16)

            @pl.loop(0, NR)
            def _(i):
                rows = pl.ds(pl.multiple_of(i * ROWS, ROWS), ROWS)
                exponent = jnp.exp(dot_nt(qr[rows, :], kr[...]) * score_scale)
                inverse = 1.0 / jnp.sum(exponent, axis=1, keepdims=True)
                if keep:
                    linv[rows, :] = jnp.broadcast_to(inverse, (ROWS, HEAD))
                prob = (exponent * inverse).astype(bf16)
                out(rows, dot(prob, vv[...]).astype(bf16))

        def to_a(rows, x):
            att_a[rows, :] = x

        def to_fake(rows, x):
            fa[rows, :] = x

        def to_guided(rows, x):
            gt[rows, :] = (
                guidance * att_a[rows, :].astype(f32) - (guidance - 1.0) * x.astype(f32)
            ).astype(bf16)

        for c in w_copies[4:]:
            c.wait()

        @pl.loop(0, NR)
        def _(i):
            pbuf[i, :, 512:768] = dot(noisy[i], wall[:, 512:768])

        attention(384, 0, rc, tqk, False, to_a)
        attention(384, 1, rn, tqk, False, to_guided)
        tokens(gt, ag, EU)
        attention(0, 0, rc, cqk, True, to_fake)
        tokens(fa, ac, EA)
        weights(tout_h, wtx, ET)

    pl.run_scoped(
        forward_phase,
        pltpu.VMEM((D, 6 * HEAD), bf16),
        pltpu.VMEM((NR, BLK, 6 * HEAD), f32),
        pltpu.VMEM((LEN, HEAD), bf16),
    )

    noise = level[0:1, 0:1]

    def later_phase(gaout, ogout, cot, diff_out, abs_out, qgout, qgown, ga, gk, gv, rg, rgt, og8):
        tile_cols = pl.ds(pl.multiple_of(myc * COLS, COLS), COLS)
        wait_bytes(gen, rsem.at[EG])
        wait_bytes(wcx, rsem.at[EW])
        wait_bytes(ac, rsem.at[EA])

        def predictions(i, total, guided):
            rows = pl.ds(pl.multiple_of(i * 128, 128), 128)
            latent = noisy[myr, rows, tile_cols].astype(f32)
            cond = latent + caps[0:1, tile_cols]
            if guided:
                null = latent + caps[1:2, tile_cols]
                velocity = guidance * cond - (guidance - 1.0) * null + total
            else:
                velocity = cond + total
            return latent - noise * velocity

        @pl.loop(0, 2)
        def _(i):
            rows = pl.ds(pl.multiple_of(i * 128, 128), 128)
            fake_pred = predictions(i, dot(ac[rows, :], wcx[...]), False)
            target = gen[rows, :].astype(f32)
            cot[rows, :] = (-noise * (fake_pred - target) * (1.0 / 64.0)).astype(bf16)
            diff_out[rows, :] = fake_pred

        @pl.loop(0, 8)
        def _(j):
            part = dot_nt(cot[...], wcx[pl.ds(pl.multiple_of(j * 512, 512), 512), :])
            for m in range(4):
                gaout[j * 4 + m] = part[:, m * HEAD : (m + 1) * HEAD].astype(bf16)

        def blocks(src, dst, e):
            @pl.loop(1, NB)
            def _(k):
                q = peer(k)
                send(src.at[q], dst.at[me], e, plane(q))

            local(src.at[me], dst.at[me], rsem.at[e])

        blocks(gaout, gain_in, EB)

        @pl.loop(0, 8)
        def _(j):
            part = dot_tn(ac[:, pl.ds(pl.multiple_of(j * 512, 512), 512)], cot[...])
            for m in range(4):
                ogout[j * 4 + m] = part[m * HEAD : (m + 1) * HEAD, :].astype(bf16)

        blocks(ogout, ogin_h, EO)

        wait_bytes(gain_in, rsem.at[EB])

        @pl.loop(0, NR)
        def _(i):
            total = jnp.zeros((ROWS, HEAD), f32)
            for c in range(8):
                total += gain_in[(c // 2) * 8 + i * 2 + c % 2].astype(f32)
            ga[pl.ds(pl.multiple_of(i * ROWS, ROWS), ROWS), :] = total.astype(bf16)

        gk[...] = jnp.zeros_like(gk)
        gv[...] = jnp.zeros_like(gv)

        def undo(rows, raw_ref, inv_ref, gain, grad):
            turned = grad * cos[rows, :] + half_turn(grad * sin[rows, :])
            scaled = gain * turned
            raw = raw_ref[rows, :]
            inverse = inv_ref[rows, :]
            back = inverse * scaled - raw * inverse * inverse * inverse * jnp.mean(
                scaled * raw, axis=1, keepdims=True
            )
            return back.astype(bf16).astype(f32)

        @pl.loop(0, NR)
        def _(i):
            rows = pl.ds(pl.multiple_of(i * ROWS, ROWS), ROWS)
            inverse = linv[rows, :][:, 0:1]
            prob = jnp.exp(dot_nt(qr[rows, :], kr[...]) * score_scale) * inverse
            grads = ga[rows, :]
            grad_prob = dot_nt(grads, vv[...])
            mean = jnp.sum(grad_prob * prob, axis=1, keepdims=True)
            grad_score = (prob * (grad_prob - mean) * score_scale).astype(bf16)
            gq = dot(grad_score, kr[...])
            gk[...] += dot_tn(qr[rows, :], grad_score)
            gv[...] += dot_tn(grads, prob.astype(bf16))
            rg[rows, 0:HEAD] = rc[i] * undo(rows, qraw, invq, cqk[0:1, :], gq)

        for i in range(NR):
            rows = pl.ds(i * ROWS, ROWS)
            grad_k = gk[:, i * ROWS : (i + 1) * ROWS].T
            grad_v = gv[:, i * ROWS : (i + 1) * ROWS].T
            rg[rows, HEAD : 2 * HEAD] = rc[i] * undo(rows, kraw, invk, cqk[1:2, :], grad_k)
            rg[rows, 2 * HEAD :] = rc[i] * grad_v.astype(bf16).astype(f32)

        for i in range(NR):
            for m in range(3):
                rgt[m * HEAD : (m + 1) * HEAD, i * ROWS : (i + 1) * ROWS] = (
                    rg[i * ROWS : (i + 1) * ROWS, m * HEAD : (m + 1) * HEAD].T.astype(bf16)
                )
        row_sum = jnp.sum(rgt[...].astype(f32), axis=1, keepdims=True)

        def share(target, put):
            @pl.loop(0, FEAT // 256)
            def _(j):
                cols = pl.ds(pl.multiple_of(target * FEAT + j * 256, 256), 256)
                total = row_sum * caps[0:1, cols]
                for i in range(NR):
                    total += dot(rgt[:, i * ROWS : (i + 1) * ROWS], noisy[i, 0:ROWS, cols])
                put(pl.ds(pl.multiple_of(j * 256, 256), 256), total * cgain[0:1, cols])

        for off in (2, 1, 3):
            target = lax.rem(w + off, 4)

            def put(cols, x, off=off):
                qgout[off - 1, :, cols] = x.astype(bf16)

            share(target, put)
            send(qgout.at[off - 1], qgin.at[off - 1], EQ, {"rep": target})

        def put_own(cols, x):
            qgown[:, cols] = x

        share(w, put_own)

        wait_bytes(ogin_h, rsem.at[EO])
        wait_bytes(ogout.at[pl.ds(0, NB - 1)], ssem.at[EO])
        pltpu.sync_copy(ogin_h, ogout)

        def og_share(target, put):
            for half in range(2):
                total = jnp.zeros((HEAD, COLS), f32)
                for r in range(NR):
                    total += ogout[target * 8 + r * 2 + half].astype(f32)
                put(pl.ds(half * COLS, COLS), total)

        for off in (2, 1, 3):
            target = lax.rem(w + off, 4)

            def put8(cols, x, off=off):
                og8[off - 1, :, cols] = x.astype(bf16)

            og_share(target, put8)
            send(og8.at[off - 1], og8in.at[off - 1], E8, {"rep": target})

        wait_bytes(wtx, rsem.at[ET])
        wait_bytes(ag, rsem.at[EU])
        abs_out[...] = jnp.zeros_like(abs_out)

        @pl.loop(0, 2)
        def _(i):
            rows = pl.ds(pl.multiple_of(i * 128, 128), 128)
            real_pred = predictions(i, dot(ag[rows, :], wtx[...]), True)
            target = gen[rows, :].astype(f32)
            gap = jnp.abs(real_pred - target)
            lanes = gap[:, 0:128]
            for j in range(1, COLS // 128):
                lanes += gap[:, j * 128 : (j + 1) * 128]
            eight = lanes[0:8, :]
            for j in range(1, 16):
                eight += lanes[j * 8 : (j + 1) * 8, :]
            abs_out[...] += eight
            cot[rows, :] = (diff_out[rows, :] - real_pred).astype(bf16)

        @pl.loop(1, NB)
        def _(k):
            send(abs_out, abs_in.at[me], ES, plane(peer(k)))

        local(abs_out, abs_in.at[me], rsem.at[ES])

        def diff_rows(t):
            return cot.at[pl.ds(pl.multiple_of(lax.rem(t, 2) * 128, 128), 128), :]

        diff_mine = diff_in.at[:, tile_cols]

        @pl.loop(1, 8)
        def _(k):
            t = lax.rem(myc + k, 8)
            send(
                diff_rows(t), diff_mine, ED,
                {"branch": t // 2, "seq": myr * 2 + lax.rem(t, 2)},
            )

        local(diff_rows(myc), diff_mine, rsem.at[ED])
        wait_bytes(abs_in, rsem.at[ES])
        wait_bytes(diff_in, rsem.at[ED])
        spread = jnp.sum(jnp.sum(abs_in[...], axis=0), axis=(0, 1), keepdims=True) * (
            1.0 / (LEN * D)
        )
        factor = 1.0 / (spread + 1e-05)

        @pl.loop(0, 8)
        def _(j):
            cols = pl.ds(pl.multiple_of(j * COLS, COLS), COLS)
            diff_in[:, cols] = (diff_in[:, cols].astype(f32) * factor).astype(bf16)

        gg_copy = local(diff_in, gg_h, lsem.at[17])

        wait_bytes(qgin, rsem.at[EQ])

        def sum_q(out):
            for m in range(3):
                for j in range(FEAT // 256):
                    rows = slice(m * HEAD, (m + 1) * HEAD)
                    cols = slice(j * 256, (j + 1) * 256)
                    total = qgown[rows, cols]
                    for off in range(3):
                        total += qgin[off, rows, cols].astype(f32)
                    out[m, j * 256 : (j + 1) * 256, :] = total.T
            local(out, qg_h, lsem.at[18]).wait()

        pl.run_scoped(sum_q, pltpu.VMEM((3, FEAT, HEAD), f32))
        wait_bytes(og8in, rsem.at[E8])

        def sum_o(out):
            def put_out(cols, x):
                total = x
                for off in range(3):
                    total += og8in[off, :, cols].astype(f32)
                out[:, cols] = total

            og_share(w, put_out)
            local(out, og_h, lsem.at[19]).wait()

        pl.run_scoped(sum_o, pltpu.VMEM((HEAD, FEAT), f32))
        gg_copy.wait()

        wait_bytes(wcx.at[pl.ds(0, (NB - 1) * HEAD), :], ssem.at[EW])
        wait_bytes(wtx.at[pl.ds(0, (NB - 1) * HEAD), :], ssem.at[ET])
        wait_bytes(gen_rows, ssem.at[EG])
        wait_bytes(ac.at[:, pl.ds(0, (NB - 1) * HEAD)], ssem.at[EA])
        wait_bytes(ag.at[:, pl.ds(0, (NB - 1) * HEAD)], ssem.at[EU])
        wait_bytes(gain_in.at[pl.ds(0, NB - 1)], ssem.at[EB])
        wait_bytes(abs_in.at[pl.ds(0, NB - 1)], ssem.at[ES])
        wait_bytes(diff_in.at[:, pl.ds(0, 7 * COLS)], ssem.at[ED])
        wait_bytes(qgin, ssem.at[EQ])
        wait_bytes(og8in, ssem.at[E8])

    pl.run_scoped(
        later_phase,
        pltpu.VMEM((NB, ROWS, HEAD), bf16),
        pltpu.VMEM((NB, HEAD, COLS), bf16),
        pltpu.VMEM((ROWS, COLS), bf16),
        pltpu.VMEM((ROWS, COLS), f32),
        pltpu.VMEM((8, 128), f32),
        pltpu.VMEM((3, 3 * HEAD, FEAT), bf16),
        pltpu.VMEM((3 * HEAD, FEAT), f32),
        pltpu.VMEM((LEN, HEAD), bf16),
        pltpu.VMEM((HEAD, LEN), f32),
        pltpu.VMEM((HEAD, LEN), f32),
        pltpu.VMEM((LEN, 3 * HEAD), f32),
        pltpu.VMEM((3 * HEAD, LEN), bf16),
        pltpu.VMEM((3, HEAD, FEAT), bf16),
    )


def body(
    noisy, generated, caption, null_caption, caption_drop, timestep, window_start,
    teacher_qkv, teacher_out, teacher_gain, teacher_qk_gain,
    critic_qkv, critic_out, critic_gain, critic_qk_gain,
):
    fraction = (timestep.astype(f32) + 1.0) / 1001.0
    noise_level = 5.0 * fraction / (1.0 + 4.0 * fraction)
    used_caption = jnp.where(caption_drop[0] == 1, null_caption, caption[0])
    caps16 = jnp.zeros((PAD, D), bf16).at[0].set(used_caption).at[1].set(null_caption)
    caps = jnp.concatenate([caps16[0:8].astype(f32)], axis=0)
    cosine, sine = rope_tables(window_start[0])
    wc = (critic_qkv.astype(f32) * critic_gain[None, :, None]).astype(bf16)
    wt = (teacher_qkv.astype(f32) * teacher_gain[None, :, None]).astype(bf16)
    level = jnp.broadcast_to(noise_level[:, None], (8, 128))
    hbm = pl.BlockSpec(memory_space=pl.ANY)
    vmem = pl.BlockSpec(memory_space=pltpu.VMEM)
    gg, qg, og, unused = pl.pallas_call(
        step_kernel,
        name="generator_step",
        out_shape=(
            jax.ShapeDtypeStruct((128, D), bf16),
            jax.ShapeDtypeStruct((3, FEAT, HEAD), f32),
            jax.ShapeDtypeStruct((HEAD, FEAT), f32),
            jax.ShapeDtypeStruct((NB, HEAD, COLS), bf16),
        ),
        in_specs=[hbm] * 6 + [vmem] * 5 + [hbm] * 3,
        out_specs=(hbm, hbm, hbm, hbm),
        scratch_shapes=[
            pltpu.VMEM((NR, BLK, D), bf16),
            pltpu.VMEM((NB * HEAD, COLS), bf16),
            pltpu.VMEM((NB * HEAD, COLS), bf16),
            pltpu.VMEM((ROWS, NB * HEAD), bf16),
            pltpu.VMEM((ROWS, NB * HEAD), bf16),
            pltpu.VMEM((NB, ROWS, HEAD), bf16),
            pltpu.VMEM((3, 3 * HEAD, FEAT), bf16),
            pltpu.VMEM((3, HEAD, FEAT), bf16),
            pltpu.VMEM((128, D), bf16),
            pltpu.VMEM((NB, 8, 128), f32),
            pltpu.VMEM((ROWS, COLS), bf16),
            pltpu.VMEM((LEN, HEAD), f32),
            pltpu.VMEM((LEN, HEAD), f32),
            pltpu.VMEM((LEN, HEAD), f32),
            pltpu.VMEM((LEN, HEAD), f32),
            pltpu.VMEM((LEN, HEAD), bf16),
            pltpu.VMEM((LEN, HEAD), bf16),
            pltpu.VMEM((LEN, HEAD), bf16),
            pltpu.VMEM((NR, ROWS, HEAD), f32),
            pltpu.VMEM((NR, ROWS, HEAD), f32),
            pltpu.VMEM((LEN, HEAD), f32),
            pltpu.VMEM((LEN, HEAD), f32),
            pltpu.VMEM((LEN, HEAD), f32),
            pltpu.VMEM((LEN, HEAD), bf16),
            pltpu.VMEM((LEN, HEAD), bf16),
            pltpu.SemaphoreType.DMA((20,)),
            pltpu.SemaphoreType.DMA((11,)),
            pltpu.SemaphoreType.DMA((11,)),
        ],
        compiler_params=pltpu.CompilerParams(
            collective_id=0, has_side_effects=True, vmem_limit_bytes=64 * 1024 * 1024
        ),
    )(
        noisy[0], wc, wt, caps16, cosine, sine, critic_qk_gain, teacher_qk_gain, level, caps,
        critic_gain[None, :], generated[0], critic_out, teacher_out,
    )
    return (gg[None], qg, og)


def solution(mesh):
    in_specs = (
        P("rep", None, None),
        P("rep", "seq", None),
        P("rep", None),
        P(),
        P("rep"),
        P("rep"),
        P("rep"),
        P(None, None, ("branch", "seq")),
        P(("branch", "seq"), None),
        P(),
        P(None, ("branch", "seq")),
        P(None, None, ("branch", "seq")),
        P(("branch", "seq"), None),
        P(),
        P(None, ("branch", "seq")),
    )
    out_specs = (
        P("rep", "seq", None),
        P(None, "rep", ("branch", "seq")),
        P(("branch", "seq"), "rep"),
    )
    return jax.shard_map(body, mesh=mesh, in_specs=in_specs, out_specs=out_specs, check_vma=False)
```

time: 642 us -> 335 us (0.52); the launches traced: 633 us -> 334 us
  waiting for transfers between devices: 412 us -> 0 us
  Pallas kernels: 0 us -> 309 us
  matrix products: 96.4 us -> 0 us
  other arithmetic: 73.1 us -> 15.9 us
  between operations: 17.8 us -> 2.73 us
  blocking collectives: 13.4 us -> 0 us
  local copies, waits for them, and re-layouts: 19.4 us -> 6.38 us
    pallas_call x0 -> x1, Pallas kernels: none -> 309 us  [body(): pl.pallas_call(step_kernel, name='generator_step', out_shape=(jax.ShapeDt...]
    reduce_scatter x3 -> x0, waiting for transfers between devices: 248 us -> none  [the longest x1 214 us: body(): lax.psum_scatter(jnp.stack([guidance * cond_part - (guidance - 1.0) * nul...]
    all_gather x1 -> x0, waiting for transfers between devices: 111 us -> none  [body(): slab_rows = lax.all_gather(cotangent_rows, 'seq', axis=1, tiled=True)]
    dot_general x14 -> x0, matrix products: 76.6 us -> none  [the longest x3 18.2 us: head_forward(): jnp.einsum('bqhe,bkhe->bhqk', rope_query, rope_key, preferred_element_typ...]
    psum x1 -> x0, waiting for transfers between devices: 53.9 us -> none  [body(): summed = lax.psum(seq_summed, 'branch').astype(jnp.float32)]
    convert_element_type x7 -> x2, other arithmetic: 33 us -> 7.8 us  [the longest x1 7.11 us: body(): wt = (teacher_qkv.astype(f32) * teacher_gain[None, :, None]).astype(bf16)]
    another operation x2 -> x0, other arithmetic: 20.6 us -> none  [the longest x1 17.2 us: body(): jnp.stack([guidance * cond_part - (guidance - 1.0) * null_part, fake_part...]
    unnamed x3 -> x0, matrix products: 19.8 us -> none
  transfers between devices with their start and end apart: 5 -> 0, of which waited for: 4 -> 0; matrix products, arithmetic and copies ran while one was open for 6% -> 0% of each run, Pallas kernels for 0% -> 0%
where the time goes in v1:
time: 335 us; the launch traced here: 334 us
  Pallas kernels  309 us (92%)
  other arithmetic  15.9 us (5%)
  local copies, waits for them, and re-layouts  6.38 us (2%)
    pallas_call x1, Pallas kernels, body(): pl.pallas_call(step_kernel, name='generator_step', out_shape=(jax.ShapeDt...  309 us
    convert_element_type x1, other arithmetic, body(): wt = (teacher_qkv.astype(f32) * teacher_gain[None, :, None]).astype(bf16)  7.11 us

profile of v1, /device:TPU:1, one launch (start us, length us, event | category | flops | bytes accessed | tf_op | source)
XLA Modules:
  0.0 334.1 jit_solution(4038728543328648548)
XLA Ops:
  0.6 0.0 copy-start.4
  0.6 0.0 copy-start.5
  2.7 0.6 broadcast_in_dim.79.level
  3.3 0.8 reduce.4
  4.1 0.7 broadcast_select_fusion
  4.9 0.7 reshape.119
  5.6 0.3 scatter.9.caps_h
  5.9 0.0 copy-start.2
  5.9 0.0 copy-start
  5.9 0.7 slice_convert_fusion.caps
  6.6 4.5 %fusion.2 = (f32[1024,64]{1,0:T(8,128)S(1)}, f32[1024,64]{1,0:T(8,128)S(1)}, f32[1024,64]{1,0:T(8,128)S(1)}) fusion(f32[64]{0:T(128)S(1)} %fusion.6, s32[1024]{0:T(1024)S(1)} %multiply_subtract_fusion, s32[1024]{0:T(1024)S(1)} %get-tuple-element.36, pred[64]{0:T(512)(128)(4,1)S(1)} %get-tuple-element.38, s32[1024]{0:T(1024)S(1)} %get-tuple-element.37, ...), kind=kLoop, calls=%fused_computation.8 | loop fusion | flops 327680 | bytes 799104 | tf_op jit(solution)/shard_map/neg | solution.py:54
  11.1 1.0 pad_maximum_fusion.1.sin_h
  12.1 1.0 pad_maximum_fusion.cos_h
  13.1 0.0 copy-done.4
  13.1 0.0 copy-done.5
  13.1 0.0 copy-done
  13.1 7.1 %multiply_convert_fusion = (bf16[3,5120,128]{2,1,0:T(8,128)(2,1)}, bf16[3,5120,128]{2,1,0:T(8,128)(2,1)}) fusion(bf16[3,5120,128]{2,1,0:T(8,128)(2,1)S(1)} %copy-done, f32[5120]{0:T(1024)S(1)} %copy-done.5, f32[5120]{0:T(1024)S(1)} %copy-done.4, bf16[3,5120,128]{2,1,0:T(8,128)(2,1)} %param.30), kind=kLoop, calls=%fused_computation | loop fusion | flops 11796480 | bytes 15769600 | tf_op jit(solution)/shard_map/convert_element_type | solution.py:537
  20.3 0.0 copy-done.2
  20.3 309.1 %generator_step.1 = (bf16[128,5120]{1,0:T(8,128)(2,1)}, f32[3,1280,128]{2,1,0:T(8,128)}, f32[128,1280]{1,0:T(8,128)}, bf16[32,128,640]{2,1,0:T(8,128)(2,1)}) custom-call(bf16[1024,5120]{1,0:T(8,128)(2,1)} %bitcast.9, bf16[3,5120,128]{2,1,0:T(8,128)(2,1)} %get-tuple-element.41.wc_h, bf16[3,5120,128]{2,1,0:T(8,128)(2,1)} %get-tuple-element.40.wt_h, ...), custom_call_target="tpu_custom_call" | custom-call | tf_op jit(solution)/shard_map/generator_step/pallas_call | solution.py:541
  329.3 0.0 copy-start.1
  329.3 2.6 copy.25
  331.9 0.0 copy-done.1
  332.0 1.3 copy.26
  333.2 0.8 copy.27
  (8 shorter events, 0.1 us)
Async XLA Ops:
  0.6 12.5 %copy-start.4 = (f32[5120]{0:T(1024)S(1)}, f32[5120]{0:T(1024)}, u32[]{:S(2)}) copy-start(f32[5120]{0:T(1024)} %param.32) | copy-start | bytes 61444
  0.6 12.5 %copy-start.5 = (f32[5120]{0:T(1024)S(1)}, f32[5120]{0:T(1024)}, u32[]{:S(2)}) copy-start(f32[5120]{0:T(1024)} %param.28) | copy-start | bytes 61444
  5.9 14.4 %copy-start.2 = (bf16[16,5120]{1,0:T(8,128)(2,1)}, bf16[16,5120]{1,0:T(8,128)(2,1)S(1)}, u32[]{:S(2)}) copy-start(bf16[16,5120]{1,0:T(8,128)(2,1)S(1)} %scatter.9.caps_h) | copy-start | bytes 491524
  5.9 7.2 %copy-start = (bf16[3,5120,128]{2,1,0:T(8,128)(2,1)S(1)}, bf16[3,5120,128]{2,1,0:T(8,128)(2,1)}, u32[]{:S(2)}) copy-start(bf16[3,5120,128]{2,1,0:T(8,128)(2,1)} %param.26) | copy-start | bytes 11796484
  329.3 2.6 copy-start.1
  329.3 3.9 %copy-start.3 = (f32[128,1280]{1,0:T(8,128)S(1)}, f32[128,1280]{1,0:T(8,128)}, u32[]{:S(2)}) copy-start(f32[128,1280]{1,0:T(8,128)} %get-tuple-element.47) | copy-start | bytes 1966084

commit v2 on v1

--- a/solution.py
+++ b/solution.py
@@ -73,31 +73,51 @@
 
 def step_kernel(
     noisy_h, wc_h, wt_h, caps_h, cos_h, sin_h, cqk, tqk, level, caps, cgain, gen_h, cout_h, tout_h,
-    gg_h, qg_h, og_h, ogin_h,
-    noisy, wcx, wtx, ac, ag, gain_in, qgin, og8in, diff_in, abs_in, gen, cos, sin,
+    gg_h, qg_h, og_h,
+    noisy, wcx, wtx, ac, ag, cotf, qgin, og8in, diff_in, abs_in, gen, cos, sin,
     qraw, kraw, qr, kr, vv, rc, rn, invq, invk, linv, fa, gt,
     lsem, rsem, ssem,
 ):
     b = lax.axis_index("branch")
     s = lax.axis_index("seq")
     w = lax.axis_index("rep")
+    core = lax.rem(b, 2)
+    z_hi = b // 2
+    z_lo = s // 4
+    x_at = lax.rem(s, 4)
+    z_at = z_hi * 2 + z_lo
     me = b * 8 + s
-    myc = b * 2 + lax.rem(s, 2)
-    myr = s // 2
+    myc = z_hi * 4 + x_at
+    myr = z_lo * 2 + core
 
     def plane(q):
         return {"branch": q // 8, "seq": lax.rem(q, 8)}
 
     def col_of(q):
-        return (q // 8) * 2 + lax.rem(q, 2)
+        return (q // 16) * 4 + lax.rem(q, 4)
 
     def row_of(q):
-        return lax.rem(q, 8) // 2
+        return (lax.rem(q, 8) // 4) * 2 + lax.rem(q // 8, 2)
+
+    def tile_of(r, c):
+        return (c // 4) * 16 + lax.rem(r, 2) * 8 + (r // 2) * 4 + lax.rem(c, 4)
 
     def peer(k):
         return lax.rem(me + k, NB)
 
-    EW, EG, ET, EA, EU, EB, EO, ED, ES, EQ, E8 = range(11)
+    sibling = {"branch": b + 1 - 2 * core}
+
+    def along_x(k):
+        return {"seq": z_lo * 4 + lax.rem(x_at + k, 4)}
+
+    def along_z(k):
+        z = lax.rem(z_at + k, 4)
+        return {"branch": (z // 2) * 2 + core, "seq": lax.rem(z, 2) * 4 + x_at}
+
+    def window(k):
+        return {"rep": lax.rem(w + k, 4)}
+
+    WC1, WC2, WC3, WT1, WT2, WT3, EG, EA, EU, C1A, C1B, C2A, C2B, C3, ED, ES, EQ, E8 = range(18)
 
     def send(src, dst, e, device):
         pltpu.make_async_remote_copy(
@@ -110,8 +130,14 @@
         c.start()
         return c
 
-    def wait_bytes(ref, sem):
-        pltpu.make_async_copy(ref, ref, sem).wait()
+    def local_in(src, dst, e):
+        pltpu.make_async_copy(src, dst, rsem.at[e]).start()
+
+    def wait_in(ref, e):
+        pltpu.make_async_copy(ref, ref, rsem.at[e]).wait()
+
+    def wait_out(ref, e):
+        pltpu.make_async_copy(ref, ref, ssem.at[e]).wait()
 
     for i in range(NR):
         local(noisy_h.at[pl.ds(i * ROWS, ROWS), :], noisy.at[i, pl.ds(0, ROWS), :], lsem.at[i])
@@ -126,29 +152,50 @@
         pl.semaphore_signal(barrier, inc=1, device_id=plane(peer(k)), device_id_type=MESH)
 
     for k in range(1, 4):
-        pl.semaphore_signal(
-            barrier, inc=1, device_id={"rep": lax.rem(w + k, 4)}, device_id_type=MESH
-        )
+        pl.semaphore_signal(barrier, inc=1, device_id=window(k), device_id_type=MESH)
     pl.semaphore_wait(barrier, NB - 1 + 3)
 
-    def weights(src, dst, e):
-        mine = dst.at[pl.ds(me * HEAD, HEAD), :]
-
-        @pl.loop(1, NB)
+    quarter = pl.ds(pl.multiple_of(w * 32, 32), 32)
+    runs = [pl.ds(pl.multiple_of(z * 16 + core * 8, 8), 8) for z in range(2)]
+
+    def weights_1(src, dst, e):
+        mine = dst.at[me, quarter, :]
+
+        @pl.loop(1, 16)
         def _(k):
-            q = peer(k)
-            send(src.at[:, pl.ds(pl.multiple_of(col_of(q) * COLS, COLS), COLS)], mine, e, plane(q))
-
-        local(src.at[:, pl.ds(pl.multiple_of(myc * COLS, COLS), COLS)], mine, rsem.at[e])
-
-    weights(cout_h, wcx, EW)
-    partner = me + 1 - 2 * lax.rem(s, 2)
+            t = lax.rem(z_hi * 8 + s + k, 16)
+            q = (t // 8) * 16 + core * 8 + lax.rem(t, 8)
+            cols = pl.ds(pl.multiple_of(col_of(q) * COLS, COLS), COLS)
+            send(src.at[quarter, cols], mine, e, plane(q))
+
+        local_in(src.at[quarter, pl.ds(pl.multiple_of(myc * COLS, COLS), COLS)], mine, e)
+
+    def weights_2(dst, e):
+        wait_in(dst.at[pl.ds(0, 16), pl.ds(0, 32), :], e - 1)
+        for k in (2, 1, 3):
+            for run in runs:
+                send(dst.at[run, quarter, :], dst.at[run, quarter, :], e, window(k))
+
+    def weights_3(dst, e):
+        wait_in(dst.at[pl.ds(0, 16), pl.ds(0, 96), :], e - 1)
+        for run in runs:
+            send(dst.at[run], dst.at[run], e, sibling)
+
+    weights_1(cout_h, wcx, WC1)
+    weights_1(tout_h, wtx, WT1)
+
     gen_rows = gen.at[pl.ds(pl.multiple_of(lax.rem(s, 2) * 128, 128), 128), :]
-    send(
-        gen_h.at[:, pl.ds(pl.multiple_of(col_of(partner) * COLS, COLS), COLS)],
-        gen_rows, EG, plane(partner),
-    )
-    local(gen_h.at[:, pl.ds(pl.multiple_of(myc * COLS, COLS), COLS)], gen_rows, rsem.at[EG])
+    has_rows = x_at // 2 == core
+
+    @pl.when(has_rows)
+    def _():
+        @pl.loop(1, 4)
+        def _(k):
+            c = z_hi * 4 + lax.rem(x_at + k, 4)
+            cols = pl.ds(pl.multiple_of(c * COLS, COLS), COLS)
+            send(gen_h.at[:, cols], gen_rows, EG, along_x(k))
+
+        local_in(gen_h.at[:, pl.ds(pl.multiple_of(myc * COLS, COLS), COLS)], gen_rows, EG)
 
     def tokens(src, dst, e):
         mine = dst.at[:, pl.ds(pl.multiple_of(me * HEAD, HEAD), HEAD)]
@@ -158,9 +205,9 @@
             q = peer(k)
             send(src.at[pl.ds(pl.multiple_of(row_of(q) * ROWS, ROWS), ROWS), :], mine, e, plane(q))
 
-        local(src.at[pl.ds(pl.multiple_of(myr * ROWS, ROWS), ROWS), :], mine, rsem.at[e])
-
-    def forward_phase(wall, pbuf, att_a):
+        local_in(src.at[pl.ds(pl.multiple_of(myr * ROWS, ROWS), ROWS), :], mine, e)
+
+    def forward_phase(wall, pbuf, att_a, tq, tk, tv):
         def load_w(j):
             src = wc_h if j < 3 else wt_h
             return local(src.at[j % 3], wall.at[:, pl.ds(j * HEAD, HEAD)], lsem.at[10 + j])
@@ -197,10 +244,13 @@
                     lax.rsqrt(sum_n + norm_eps), (128, 128)
                 )
 
+        weights_2(wcx, WC2)
         cos_copy.wait()
         sin_copy.wait()
 
-        def attention(col, row, scale_ref, gains, keep, out):
+        def attention(col, row, scale_ref, gains, tables, keep, out):
+            q_ref, k_ref, v_ref = tables
+
             @pl.loop(0, NR)
             def _(i):
                 rows = pl.ds(pl.multiple_of(i * ROWS, ROWS), ROWS)
@@ -215,7 +265,9 @@
                     ]
                     return scale * (block + shift)
 
-                for m, (dst, raw_ref, inv_ref) in enumerate(((qr, qraw, invq), (kr, kraw, invk))):
+                for m, (dst, raw_ref, inv_ref) in enumerate(
+                    ((q_ref, qraw, invq), (k_ref, kraw, invk))
+                ):
                     x = raw(m)
                     inverse = lax.rsqrt(jnp.mean(x * x, axis=1, keepdims=True) + norm_eps)
                     normed = x * inverse * gains[m : m + 1, :]
@@ -223,17 +275,17 @@
                     if keep:
                         raw_ref[rows, :] = x
                         inv_ref[rows, :] = jnp.broadcast_to(inverse, (ROWS, HEAD))
-                vv[rows, :] = raw(2).astype(bf16)
+                v_ref[rows, :] = raw(2).astype(bf16)
 
             @pl.loop(0, NR)
             def _(i):
                 rows = pl.ds(pl.multiple_of(i * ROWS, ROWS), ROWS)
-                exponent = jnp.exp(dot_nt(qr[rows, :], kr[...]) * score_scale)
+                exponent = jnp.exp(dot_nt(q_ref[rows, :], k_ref[...]) * score_scale)
                 inverse = 1.0 / jnp.sum(exponent, axis=1, keepdims=True)
                 if keep:
                     linv[rows, :] = jnp.broadcast_to(inverse, (ROWS, HEAD))
                 prob = (exponent * inverse).astype(bf16)
-                out(rows, dot(prob, vv[...]).astype(bf16))
+                out(rows, dot(prob, v_ref[...]).astype(bf16))
 
         def to_a(rows, x):
             att_a[rows, :] = x
@@ -246,6 +298,9 @@
                 guidance * att_a[rows, :].astype(f32) - (guidance - 1.0) * x.astype(f32)
             ).astype(bf16)
 
+        attention(0, 0, rc, cqk, (qr, kr, vv), True, to_fake)
+        tokens(fa, ac, EA)
+        weights_2(wtx, WT2)
         for c in w_copies[4:]:
             c.wait()
 
@@ -253,27 +308,29 @@
         def _(i):
             pbuf[i, :, 512:768] = dot(noisy[i], wall[:, 512:768])
 
-        attention(384, 0, rc, tqk, False, to_a)
-        attention(384, 1, rn, tqk, False, to_guided)
+        attention(384, 0, rc, tqk, (tq, tk, tv), False, to_a)
+        attention(384, 1, rn, tqk, (tq, tk, tv), False, to_guided)
         tokens(gt, ag, EU)
-        attention(0, 0, rc, cqk, True, to_fake)
-        tokens(fa, ac, EA)
-        weights(tout_h, wtx, ET)
 
     pl.run_scoped(
         forward_phase,
         pltpu.VMEM((D, 6 * HEAD), bf16),
         pltpu.VMEM((NR, BLK, 6 * HEAD), f32),
         pltpu.VMEM((LEN, HEAD), bf16),
+        pltpu.VMEM((LEN, HEAD), bf16),
+        pltpu.VMEM((LEN, HEAD), bf16),
+        pltpu.VMEM((LEN, HEAD), bf16),
     )
 
     noise = level[0:1, 0:1]
 
-    def later_phase(gaout, ogout, cot, diff_out, abs_out, qgout, qgown, ga, gk, gv, rg, rgt, og8):
+    def later_phase(cout, diff_out, fake, abs_out, qgout, qgown, gk, gv, rgt, og8, ogown):
+        cout_copy = local(cout_h, cout, lsem.at[16])
         tile_cols = pl.ds(pl.multiple_of(myc * COLS, COLS), COLS)
-        wait_bytes(gen, rsem.at[EG])
-        wait_bytes(wcx, rsem.at[EW])
-        wait_bytes(ac, rsem.at[EA])
+        weights_3(wcx, WC3)
+        wait_in(gen, EG)
+        wait_in(ac, EA)
+        wait_in(wcx.at[pl.ds(0, 16)], WC3)
 
         def predictions(i, total, guided):
             rows = pl.ds(pl.multiple_of(i * 128, 128), 128)
@@ -286,46 +343,37 @@
                 velocity = cond + total
             return latent - noise * velocity
 
-        @pl.loop(0, 2)
-        def _(i):
-            rows = pl.ds(pl.multiple_of(i * 128, 128), 128)
-            fake_pred = predictions(i, dot(ac[rows, :], wcx[...]), False)
+        def product(att, weights, rows):
+            return dot(att[rows, :], weights[...].reshape(NB * HEAD, COLS))
+
+        def cotangent(i):
+            rows = pl.ds(i * 128, 128)
+            fake_pred = predictions(i, product(ac, wcx, rows), False)
             target = gen[rows, :].astype(f32)
-            cot[rows, :] = (-noise * (fake_pred - target) * (1.0 / 64.0)).astype(bf16)
-            diff_out[rows, :] = fake_pred
-
-        @pl.loop(0, 8)
-        def _(j):
-            part = dot_nt(cot[...], wcx[pl.ds(pl.multiple_of(j * 512, 512), 512), :])
-            for m in range(4):
-                gaout[j * 4 + m] = part[:, m * HEAD : (m + 1) * HEAD].astype(bf16)
-
-        def blocks(src, dst, e):
-            @pl.loop(1, NB)
-            def _(k):
-                q = peer(k)
-                send(src.at[q], dst.at[me], e, plane(q))
-
-            local(src.at[me], dst.at[me], rsem.at[e])
-
-        blocks(gaout, gain_in, EB)
-
-        @pl.loop(0, 8)
-        def _(j):
-            part = dot_tn(ac[:, pl.ds(pl.multiple_of(j * 512, 512), 512)], cot[...])
-            for m in range(4):
-                ogout[j * 4 + m] = part[m * HEAD : (m + 1) * HEAD, :].astype(bf16)
-
-        blocks(ogout, ogin_h, EO)
-
-        wait_bytes(gain_in, rsem.at[EB])
-
-        @pl.loop(0, NR)
-        def _(i):
-            total = jnp.zeros((ROWS, HEAD), f32)
-            for c in range(8):
-                total += gain_in[(c // 2) * 8 + i * 2 + c % 2].astype(f32)
-            ga[pl.ds(pl.multiple_of(i * ROWS, ROWS), ROWS), :] = total.astype(bf16)
+            cotf[me, rows, :] = (-noise * (fake_pred - target) * (1.0 / 64.0)).astype(bf16)
+            fake[rows, :] = fake_pred
+
+        top, low = pl.ds(0, 128), pl.ds(128, 128)
+        cotangent(0)
+        for k in (2, 1, 3):
+            send(cotf.at[me, top, :], cotf.at[me, top, :], C1A, along_x(k))
+        cotangent(1)
+        for k in (2, 1, 3):
+            send(cotf.at[me, low, :], cotf.at[me, low, :], C1B, along_z(k))
+        wait_in(cotf.at[pl.ds(0, 3), top, :], C1A)
+        x_run = pl.ds(me - x_at, 4)
+        for k in (2, 1, 3):
+            send(cotf.at[x_run, top, :], cotf.at[x_run, top, :], C2A, along_z(k))
+        wait_in(cotf.at[pl.ds(0, 3), low, :], C1B)
+        for k in (2, 1, 3):
+            for z in range(4):
+                held = cotf.at[(z // 2) * 16 + core * 8 + (z % 2) * 4 + x_at, low, :]
+                send(held, held, C2B, along_x(k))
+        cout_copy.wait()
+        wait_in(cotf.at[pl.ds(0, 12), top, :], C2A)
+        wait_in(cotf.at[pl.ds(0, 12), low, :], C2B)
+        for run in runs:
+            send(cotf.at[run], cotf.at[run], C3, sibling)
 
         gk[...] = jnp.zeros_like(gk)
         gv[...] = jnp.zeros_like(gv)
@@ -340,32 +388,59 @@
             )
             return back.astype(bf16).astype(f32)
 
-        @pl.loop(0, NR)
-        def _(i):
-            rows = pl.ds(pl.multiple_of(i * ROWS, ROWS), ROWS)
-            inverse = linv[rows, :][:, 0:1]
-            prob = jnp.exp(dot_nt(qr[rows, :], kr[...]) * score_scale) * inverse
-            grads = ga[rows, :]
-            grad_prob = dot_nt(grads, vv[...])
-            mean = jnp.sum(grad_prob * prob, axis=1, keepdims=True)
-            grad_score = (prob * (grad_prob - mean) * score_scale).astype(bf16)
-            gq = dot(grad_score, kr[...])
-            gk[...] += dot_tn(qr[rows, :], grad_score)
-            gv[...] += dot_tn(grads, prob.astype(bf16))
-            rg[rows, 0:HEAD] = rc[i] * undo(rows, qraw, invq, cqk[0:1, :], gq)
+        def backward_rows(side):
+            @pl.loop(0, 2)
+            def _(j):
+                i = j * 2 + side
+                rows = pl.ds(pl.multiple_of(i * ROWS, ROWS), ROWS)
+                total = jnp.zeros((ROWS, HEAD), f32)
+                for c in range(8):
+                    total += dot_nt(cotf[tile_of(i, c)], cout[:, c * COLS : (c + 1) * COLS])
+                grads = total.astype(bf16)
+                inverse = linv[rows, :][:, 0:1]
+                prob = jnp.exp(dot_nt(qr[rows, :], kr[...]) * score_scale) * inverse
+                grad_prob = dot_nt(grads, vv[...])
+                mean = jnp.sum(grad_prob * prob, axis=1, keepdims=True)
+                grad_score = (prob * (grad_prob - mean) * score_scale).astype(bf16)
+                gq = dot(grad_score, kr[...])
+                gk[...] += dot_tn(qr[rows, :], grad_score)
+                gv[...] += dot_tn(grads, prob.astype(bf16))
+                rg = rc[i] * undo(rows, qraw, invq, cqk[0:1, :], gq)
+                rgt[0:HEAD, rows] = rg.T.astype(bf16)
+
+        backward_rows(core)
+        wait_in(cotf.at[pl.ds(0, 16)], C3)
+
+        def og_share(target, put):
+            for half in range(2):
+                total = jnp.zeros((HEAD, COLS), f32)
+                for r in range(NR):
+                    total += dot_tn(
+                        fa[r * ROWS : (r + 1) * ROWS, :], cotf[tile_of(r, target * 2 + half)]
+                    )
+                put(pl.ds(half * COLS, COLS), total)
+
+        @pl.loop(0, 3)
+        def _(n):
+            off = lax.rem(n + 1, 3) + 1
+            target = lax.rem(w + off, 4)
+
+            def put8(cols, x):
+                og8[off - 1, :, cols] = x.astype(bf16)
+
+            og_share(target, put8)
+            send(og8.at[off - 1], og8in.at[off - 1], E8, {"rep": target})
+
+        backward_rows(1 - core)
 
         for i in range(NR):
             rows = pl.ds(i * ROWS, ROWS)
             grad_k = gk[:, i * ROWS : (i + 1) * ROWS].T
             grad_v = gv[:, i * ROWS : (i + 1) * ROWS].T
-            rg[rows, HEAD : 2 * HEAD] = rc[i] * undo(rows, kraw, invk, cqk[1:2, :], grad_k)
-            rg[rows, 2 * HEAD :] = rc[i] * grad_v.astype(bf16).astype(f32)
-
-        for i in range(NR):
-            for m in range(3):
-                rgt[m * HEAD : (m + 1) * HEAD, i * ROWS : (i + 1) * ROWS] = (
-                    rg[i * ROWS : (i + 1) * ROWS, m * HEAD : (m + 1) * HEAD].T.astype(bf16)
-                )
+            grad_k = rc[i] * undo(rows, kraw, invk, cqk[1:2, :], grad_k)
+            grad_v = rc[i] * grad_v.astype(bf16).astype(f32)
+            rgt[HEAD : 2 * HEAD, rows] = grad_k.T.astype(bf16)
+            rgt[2 * HEAD :, rows] = grad_v.T.astype(bf16)
         row_sum = jnp.sum(rgt[...].astype(f32), axis=1, keepdims=True)
 
         def share(target, put):
@@ -391,34 +466,15 @@
 
         share(w, put_own)
 
-        wait_bytes(ogin_h, rsem.at[EO])
-        wait_bytes(ogout.at[pl.ds(0, NB - 1)], ssem.at[EO])
-        pltpu.sync_copy(ogin_h, ogout)
-
-        def og_share(target, put):
-            for half in range(2):
-                total = jnp.zeros((HEAD, COLS), f32)
-                for r in range(NR):
-                    total += ogout[target * 8 + r * 2 + half].astype(f32)
-                put(pl.ds(half * COLS, COLS), total)
-
-        for off in (2, 1, 3):
-            target = lax.rem(w + off, 4)
-
-            def put8(cols, x, off=off):
-                og8[off - 1, :, cols] = x.astype(bf16)
-
-            og_share(target, put8)
-            send(og8.at[off - 1], og8in.at[off - 1], E8, {"rep": target})
-
-        wait_bytes(wtx, rsem.at[ET])
-        wait_bytes(ag, rsem.at[EU])
+        weights_3(wtx, WT3)
+        wait_in(ag, EU)
+        wait_in(wtx.at[pl.ds(0, 16)], WT3)
         abs_out[...] = jnp.zeros_like(abs_out)
 
         @pl.loop(0, 2)
         def _(i):
             rows = pl.ds(pl.multiple_of(i * 128, 128), 128)
-            real_pred = predictions(i, dot(ag[rows, :], wtx[...]), True)
+            real_pred = predictions(i, product(ag, wtx, rows), True)
             target = gen[rows, :].astype(f32)
             gap = jnp.abs(real_pred - target)
             lanes = gap[:, 0:128]
@@ -428,30 +484,36 @@
             for j in range(1, 16):
                 eight += lanes[j * 8 : (j + 1) * 8, :]
             abs_out[...] += eight
-            cot[rows, :] = (diff_out[rows, :] - real_pred).astype(bf16)
+            diff_out[rows, :] = (fake[rows, :] - real_pred).astype(bf16)
 
         @pl.loop(1, NB)
         def _(k):
             send(abs_out, abs_in.at[me], ES, plane(peer(k)))
 
-        local(abs_out, abs_in.at[me], rsem.at[ES])
-
-        def diff_rows(t):
-            return cot.at[pl.ds(pl.multiple_of(lax.rem(t, 2) * 128, 128), 128), :]
+        local_in(abs_out, abs_in.at[me], ES)
 
         diff_mine = diff_in.at[:, tile_cols]
 
-        @pl.loop(1, 8)
-        def _(k):
-            t = lax.rem(myc + k, 8)
-            send(
-                diff_rows(t), diff_mine, ED,
-                {"branch": t // 2, "seq": myr * 2 + lax.rem(t, 2)},
-            )
-
-        local(diff_rows(myc), diff_mine, rsem.at[ED])
-        wait_bytes(abs_in, rsem.at[ES])
-        wait_bytes(diff_in, rsem.at[ED])
+        @pl.loop(0, 8)
+        def _(t):
+            e = lax.rem(t, 2)
+            to_b = t // 2
+            to_s = myr * 2 + e
+            src = diff_out.at[pl.ds(pl.multiple_of(e * 128, 128), 128), :]
+            mine = to_b * 8 + to_s == me
+
+            @pl.when(mine)
+            def _():
+                local_in(src, diff_mine, ED)
+
+            @pl.when(jnp.logical_not(mine))
+            def _():
+                send(src, diff_mine, ED, {"branch": to_b, "seq": to_s})
+
+        og_share(w, lambda cols, x: ogown.__setitem__((slice(None), cols), x))
+
+        wait_in(abs_in, ES)
+        wait_in(diff_in, ED)
         spread = jnp.sum(jnp.sum(abs_in[...], axis=0), axis=(0, 1), keepdims=True) * (
             1.0 / (LEN * D)
         )
@@ -464,7 +526,15 @@
 
         gg_copy = local(diff_in, gg_h, lsem.at[17])
 
-        wait_bytes(qgin, rsem.at[EQ])
+        wait_in(og8in, E8)
+        for j in range(5):
+            cols = slice(j * 256, (j + 1) * 256)
+            total = ogown[:, cols]
+            for off in range(3):
+                total += og8in[off, :, cols].astype(f32)
+            ogown[:, cols] = total
+        og_copy = local(ogown, og_h, lsem.at[19])
+        wait_in(qgin, EQ)
 
         def sum_q(out):
             for m in range(3):
@@ -478,47 +548,51 @@
             local(out, qg_h, lsem.at[18]).wait()
 
         pl.run_scoped(sum_q, pltpu.VMEM((3, FEAT, HEAD), f32))
-        wait_bytes(og8in, rsem.at[E8])
-
-        def sum_o(out):
-            def put_out(cols, x):
-                total = x
-                for off in range(3):
-                    total += og8in[off, :, cols].astype(f32)
-                out[:, cols] = total
-
-            og_share(w, put_out)
-            local(out, og_h, lsem.at[19]).wait()
-
-        pl.run_scoped(sum_o, pltpu.VMEM((HEAD, FEAT), f32))
+        og_copy.wait()
         gg_copy.wait()
 
-        wait_bytes(wcx.at[pl.ds(0, (NB - 1) * HEAD), :], ssem.at[EW])
-        wait_bytes(wtx.at[pl.ds(0, (NB - 1) * HEAD), :], ssem.at[ET])
-        wait_bytes(gen_rows, ssem.at[EG])
-        wait_bytes(ac.at[:, pl.ds(0, (NB - 1) * HEAD)], ssem.at[EA])
-        wait_bytes(ag.at[:, pl.ds(0, (NB - 1) * HEAD)], ssem.at[EU])
-        wait_bytes(gain_in.at[pl.ds(0, NB - 1)], ssem.at[EB])
-        wait_bytes(abs_in.at[pl.ds(0, NB - 1)], ssem.at[ES])
-        wait_bytes(diff_in.at[:, pl.ds(0, 7 * COLS)], ssem.at[ED])
-        wait_bytes(qgin, ssem.at[EQ])
-        wait_bytes(og8in, ssem.at[E8])
+        for dst, e in ((wcx, WC1), (wtx, WT1)):
+            wait_out(dst.at[pl.ds(0, 15), pl.ds(0, 32), :], e)
+            wait_out(dst.at[pl.ds(0, 16), pl.ds(0, 96), :], e + 1)
+            wait_out(dst.at[pl.ds(0, 16)], e + 2)
+
+        @pl.when(has_rows)
+        def _():
+            wait_out(diff_in.at[:, pl.ds(0, 3 * COLS)], EG)
+
+        wait_out(ac.at[:, pl.ds(0, (NB - 1) * HEAD)], EA)
+        wait_out(ag.at[:, pl.ds(0, (NB - 1) * HEAD)], EU)
+        wait_out(cotf.at[pl.ds(0, 3), top, :], C1A)
+        wait_out(cotf.at[pl.ds(0, 3), low, :], C1B)
+        wait_out(cotf.at[pl.ds(0, 12), top, :], C2A)
+        wait_out(cotf.at[pl.ds(0, 12), low, :], C2B)
+        wait_out(cotf.at[pl.ds(0, 16)], C3)
+        wait_out(abs_in.at[pl.ds(0, NB - 1)], ES)
+
+        @pl.when(has_rows)
+        def _():
+            wait_out(diff_in.at[:, pl.ds(0, 7 * COLS)], ED)
+
+        @pl.when(jnp.logical_not(has_rows))
+        def _():
+            wait_out(diff_in, ED)
+
+        wait_out(qgin, EQ)
+        wait_out(og8in, E8)
 
     pl.run_scoped(
         later_phase,
-        pltpu.VMEM((NB, ROWS, HEAD), bf16),
-        pltpu.VMEM((NB, HEAD, COLS), bf16),
+        pltpu.VMEM((HEAD, D), bf16),
         pltpu.VMEM((ROWS, COLS), bf16),
         pltpu.VMEM((ROWS, COLS), f32),
         pltpu.VMEM((8, 128), f32),
         pltpu.VMEM((3, 3 * HEAD, FEAT), bf16),
         pltpu.VMEM((3 * HEAD, FEAT), f32),
-        pltpu.VMEM((LEN, HEAD), bf16),
         pltpu.VMEM((HEAD, LEN), f32),
         pltpu.VMEM((HEAD, LEN), f32),
-        pltpu.VMEM((LEN, 3 * HEAD), f32),
         pltpu.VMEM((3 * HEAD, LEN), bf16),
         pltpu.VMEM((3, HEAD, FEAT), bf16),
+        pltpu.VMEM((HEAD, FEAT), f32),
     )
 
 
@@ -538,24 +612,23 @@
     level = jnp.broadcast_to(noise_level[:, None], (8, 128))
     hbm = pl.BlockSpec(memory_space=pl.ANY)
     vmem = pl.BlockSpec(memory_space=pltpu.VMEM)
-    gg, qg, og, unused = pl.pallas_call(
+    gg, qg, og = pl.pallas_call(
         step_kernel,
         name="generator_step",
         out_shape=(
             jax.ShapeDtypeStruct((128, D), bf16),
             jax.ShapeDtypeStruct((3, FEAT, HEAD), f32),
             jax.ShapeDtypeStruct((HEAD, FEAT), f32),
-            jax.ShapeDtypeStruct((NB, HEAD, COLS), bf16),
         ),
         in_specs=[hbm] * 6 + [vmem] * 5 + [hbm] * 3,
-        out_specs=(hbm, hbm, hbm, hbm),
+        out_specs=(hbm, hbm, hbm),
         scratch_shapes=[
             pltpu.VMEM((NR, BLK, D), bf16),
-            pltpu.VMEM((NB * HEAD, COLS), bf16),
-            pltpu.VMEM((NB * HEAD, COLS), bf16),
+            pltpu.VMEM((NB, HEAD, COLS), bf16),
+            pltpu.VMEM((NB, HEAD, COLS), bf16),
             pltpu.VMEM((ROWS, NB * HEAD), bf16),
             pltpu.VMEM((ROWS, NB * HEAD), bf16),
-            pltpu.VMEM((NB, ROWS, HEAD), bf16),
+            pltpu.VMEM((NB, ROWS, COLS), bf16),
             pltpu.VMEM((3, 3 * HEAD, FEAT), bf16),
             pltpu.VMEM((3, HEAD, FEAT), bf16),
             pltpu.VMEM((128, D), bf16),
@@ -576,8 +649,8 @@
             pltpu.VMEM((LEN, HEAD), bf16),
             pltpu.VMEM((LEN, HEAD), bf16),
             pltpu.SemaphoreType.DMA((20,)),
-            pltpu.SemaphoreType.DMA((11,)),
-            pltpu.SemaphoreType.DMA((11,)),
+            pltpu.SemaphoreType.DMA((18,)),
+            pltpu.SemaphoreType.DMA((18,)),
         ],
         compiler_params=pltpu.CompilerParams(
             collective_id=0, has_side_effects=True, vmem_limit_bytes=64 * 1024 * 1024

time: 335 us -> 212 us (0.63)
  Pallas kernels: 309 us -> 187 us
    pallas_call x1, Pallas kernels: 309 us -> 187 us  [body(): pl.pallas_call(step_kernel, name='generator_step', out_shape=(jax.ShapeDt...]
where the time goes in v2:
time: 212 us
  Pallas kernels  187 us (88%)
  other arithmetic  15.7 us (7%)
  local copies, waits for them, and re-layouts  6.38 us (3%)
  between operations  2.73 us (1%)
    pallas_call x1, Pallas kernels, body(): pl.pallas_call(step_kernel, name='generator_step', out_shape=(jax.ShapeDt...  187 us
    convert_element_type x1, other arithmetic, body(): wt = (teacher_qkv.astype(f32) * teacher_gain[None, :, None]).astype(bf16)  6.94 us
    unnamed x15, local copies, waits for them, and re-layouts  4.75 us
    neg x1, other arithmetic, rope_tables(): -sine  4.52 us

profile of v2, /device:TPU:1, one launch (start us, length us, event | category | flops | bytes accessed | tf_op | source)
XLA Modules:
  0.0 211.9 jit_solution(2693080773716739119)
XLA Ops:
  0.6 0.0 copy-start.4
  0.6 0.0 copy-start.5
  2.7 0.6 broadcast_in_dim.79.level
  3.3 0.8 reduce.4
  4.1 0.7 broadcast_select_fusion
  4.9 0.7 reshape.119
  5.6 0.3 scatter.9.caps_h
  5.9 0.0 copy-start.2
  5.9 0.0 copy-start
  5.9 0.7 slice_convert_fusion.caps
  6.6 4.5 %fusion.2 = (f32[1024,64]{1,0:T(8,128)S(1)}, f32[1024,64]{1,0:T(8,128)S(1)}, f32[1024,64]{1,0:T(8,128)S(1)}) fusion(f32[64]{0:T(128)S(1)} %fusion.6, s32[1024]{0:T(1024)S(1)} %multiply_subtract_fusion, s32[1024]{0:T(1024)S(1)} %get-tuple-element.36, pred[64]{0:T(512)(128)(4,1)S(1)} %get-tuple-element.38, s32[1024]{0:T(1024)S(1)} %get-tuple-element.37, ...), kind=kLoop, calls=%fused_computation.8 | loop fusion | flops 327680 | bytes 799104 | tf_op jit(solution)/shard_map/neg | solution.py:54
  11.1 1.0 pad_maximum_fusion.1.sin_h
  12.1 1.0 pad_maximum_fusion.cos_h
  13.1 0.0 copy-done.4
  13.1 0.0 copy-done.5
  13.1 0.0 copy-done
  13.1 6.9 %multiply_convert_fusion = (bf16[3,5120,128]{2,1,0:T(8,128)(2,1)}, bf16[3,5120,128]{2,1,0:T(8,128)(2,1)}) fusion(bf16[3,5120,128]{2,1,0:T(8,128)(2,1)S(1)} %copy-done, f32[5120]{0:T(1024)S(1)} %copy-done.5, f32[5120]{0:T(1024)S(1)} %copy-done.4, bf16[3,5120,128]{2,1,0:T(8,128)(2,1)} %param.30), kind=kLoop, calls=%fused_computation | loop fusion | flops 11796480 | bytes 15769600 | tf_op jit(solution)/shard_map/convert_element_type | solution.py:611
  20.1 0.0 copy-done.2
  20.1 187.1 %generator_step.1 = (bf16[128,5120]{1,0:T(8,128)(2,1)}, f32[3,1280,128]{2,1,0:T(8,128)}, f32[128,1280]{1,0:T(8,128)}) custom-call(bf16[1024,5120]{1,0:T(8,128)(2,1)} %bitcast.9, bf16[3,5120,128]{2,1,0:T(8,128)(2,1)} %get-tuple-element.41.wc_h, bf16[3,5120,128]{2,1,0:T(8,128)(2,1)} %get-tuple-element.40.wt_h, bf16[16,5120]{1,0:T(8,128)(2,1)} %copy-done.2, ...), custom_call_target="tpu_custom_call" | custom-call | tf_op jit(solution)/shard_map/generator_step/pallas_call | solution.py:615
  207.1 0.0 copy-start.1
  207.2 0.0 copy-start.3
  207.2 2.6 %copy.25 = bf16[1,128,5120]{2,1,0:T(8,128)(2,1)} copy(bf16[1,128,5120]{2,1,0:T(8,128)(2,1)} %bitcast.11) | data formatting | bytes 2621440
  209.8 1.3 copy.26
  211.0 0.8 copy.27
  (8 shorter events, 0.1 us)
Async XLA Ops:
  0.6 12.5 %copy-start.4 = (f32[5120]{0:T(1024)S(1)}, f32[5120]{0:T(1024)}, u32[]{:S(2)}) copy-start(f32[5120]{0:T(1024)} %param.32) | copy-start | bytes 61444
  0.6 12.5 %copy-start.5 = (f32[5120]{0:T(1024)S(1)}, f32[5120]{0:T(1024)}, u32[]{:S(2)}) copy-start(f32[5120]{0:T(1024)} %param.28) | copy-start | bytes 61444
  5.9 14.2 %copy-start.2 = (bf16[16,5120]{1,0:T(8,128)(2,1)}, bf16[16,5120]{1,0:T(8,128)(2,1)S(1)}, u32[]{:S(2)}) copy-start(bf16[16,5120]{1,0:T(8,128)(2,1)S(1)} %scatter.9.caps_h) | copy-start | bytes 491524
  5.9 7.2 %copy-start = (bf16[3,5120,128]{2,1,0:T(8,128)(2,1)S(1)}, bf16[3,5120,128]{2,1,0:T(8,128)(2,1)}, u32[]{:S(2)}) copy-start(bf16[3,5120,128]{2,1,0:T(8,128)(2,1)} %param.26) | copy-start | bytes 11796484
  207.1 2.6 %copy-start.1 = (f32[3,1280,128]{2,1,0:T(8,128)S(1)}, f32[3,1280,128]{2,1,0:T(8,128)}, u32[]{:S(2)}) copy-start(f32[3,1280,128]{2,1,0:T(8,128)} %get-tuple-element.46) | copy-start | bytes 5898244
  207.2 3.9 %copy-start.3 = (f32[128,1280]{1,0:T(8,128)S(1)}, f32[128,1280]{1,0:T(8,128)}, u32[]{:S(2)}) copy-start(f32[128,1280]{1,0:T(8,128)} %get-tuple-element.47) | copy-start | bytes 1966084

commit v3 on v2

--- a/solution.py
+++ b/solution.py
@@ -26,33 +26,20 @@
 MESH = pl.DeviceIdType.MESH
 
 
-def rope_tables(first_token):
-    token_index = first_token + jnp.arange(LEN, dtype=jnp.int32)
-    plane_size = GRID_H * GRID_W
-    frame_index = token_index // plane_size
-    remainder = token_index - frame_index * plane_size
-    row_index = remainder // GRID_W
-    column_index = remainder - row_index * GRID_W
-    pair_index = jnp.arange(64, dtype=jnp.int32)
-    in_frames = pair_index < 22
-    in_rows = jnp.logical_and(pair_index >= 22, pair_index < 43)
-    local_rank = jnp.where(
-        in_frames, pair_index, jnp.where(in_rows, pair_index - 22, pair_index - 43)
-    ).astype(f32)
-    axis_width = jnp.where(in_frames, 44.0, 42.0).astype(f32)
-    frequency = jnp.exp(-jnp.log(10000.0) * 2.0 * local_rank / axis_width)
-    chosen = jnp.where(
-        in_frames[None, :],
-        frame_index[:, None],
-        jnp.where(in_rows[None, :], row_index[:, None], column_index[:, None]),
-    ).astype(f32)
-    angles = chosen * frequency[None, :]
-    cosine = jnp.cos(angles)
-    sine = jnp.sin(angles)
-    return (
-        jnp.concatenate([cosine, cosine], axis=1),
-        jnp.concatenate([-sine, sine], axis=1),
-    )
+def rope_table():
+    spot = jnp.arange(128, dtype=jnp.int32)[:, None]
+    pair = jnp.arange(64, dtype=jnp.int32)[None, :]
+    axis = jnp.where(pair < 22, 0, jnp.where(pair < 43, 1, 2))
+    first = jnp.where(axis == 0, 0, jnp.where(axis == 1, 22, 43))
+    width = jnp.where(axis == 0, 44.0, 42.0).astype(f32)
+    frequency = jnp.exp(-jnp.log(10000.0) * 2.0 * (pair - first).astype(f32) / width)
+    held = jnp.where(spot < 32, 0, jnp.where(spot < 64, 1, 2))
+    place = spot - jnp.where(held == 0, 0, jnp.where(held == 1, 32, 64))
+    angle = place.astype(f32) * frequency
+    inside = held == axis
+    cosine = jnp.where(inside, jnp.cos(angle), 0.0)
+    sine = jnp.where(inside, jnp.sin(angle), 0.0)
+    return jnp.concatenate([cosine, cosine, -sine, sine], axis=1)
 
 
 def dot(a, b):
@@ -72,10 +59,11 @@
 
 
 def step_kernel(
-    noisy_h, wc_h, wt_h, caps_h, cos_h, sin_h, cqk, tqk, level, caps, cgain, gen_h, cout_h, tout_h,
+    scalars, noisy_h, wc_h, wt_h, caption, null_caption, table, cqk, tqk, cgain, tgain,
+    gen_h, cout_h, tout_h,
     gg_h, qg_h, og_h,
-    noisy, wcx, wtx, ac, ag, cotf, qgin, og8in, diff_in, abs_in, gen, cos, sin,
-    qraw, kraw, qr, kr, vv, rc, rn, invq, invk, linv, fa, gt,
+    noisy, wcx, wtx, ac, ag, gain_in, cotf, pair, ogsib, qgin, qgfwd, og8in, diff_in, abs_in, gen,
+    cos, sin, caps, qraw, kraw, qr, kr, vv, rc, rn, invq, invk, linv, fa, gt,
     lsem, rsem, ssem,
 ):
     b = lax.axis_index("branch")
@@ -117,7 +105,10 @@
     def window(k):
         return {"rep": lax.rem(w + k, 4)}
 
-    WC1, WC2, WC3, WT1, WT2, WT3, EG, EA, EU, C1A, C1B, C2A, C2B, C3, ED, ES, EQ, E8 = range(18)
+    (
+        WC1, WC2, WC3, WT1, WT2, WT3, EG, EA, EU, EB, C1A, C1B, C2A, C2B, FX, CS,
+        ED, ES, QF0, QF1, QD0, QD1, QC0, QC1, E8,
+    ) = range(25)
 
     def send(src, dst, e, device):
         pltpu.make_async_remote_copy(
@@ -141,9 +132,6 @@
 
     for i in range(NR):
         local(noisy_h.at[pl.ds(i * ROWS, ROWS), :], noisy.at[i, pl.ds(0, ROWS), :], lsem.at[i])
-    cap_copies = [local(caps_h, noisy.at[i, pl.ds(ROWS, PAD), :], lsem.at[4 + i]) for i in range(NR)]
-    cos_copy = local(cos_h, cos, lsem.at[8])
-    sin_copy = local(sin_h, sin, lsem.at[9])
 
     barrier = pltpu.get_barrier_semaphore()
 
@@ -207,17 +195,59 @@
 
         local_in(src.at[pl.ds(pl.multiple_of(myr * ROWS, ROWS), ROWS), :], mine, e)
 
-    def forward_phase(wall, pbuf, att_a, tq, tk, tv):
+    def forward_phase(wall, pbuf, tq, tk, tv):
         def load_w(j):
             src = wc_h if j < 3 else wt_h
             return local(src.at[j % 3], wall.at[:, pl.ds(j * HEAD, HEAD)], lsem.at[10 + j])
 
         w_copies = [load_w(j) for j in range(6)]
 
-        for c in cap_copies:
-            c.wait()
+        dropped = jnp.full((40, 128), scalars[0, 0], jnp.int32) == 1
+        null = null_caption[...]
+        used = jnp.where(dropped, null, caption[...])
+        caps[...] = jnp.zeros_like(caps)
+        for j in range(40):
+            caps[0:1, j * 128 : (j + 1) * 128] = used[j : j + 1, :]
+            caps[1:2, j * 128 : (j + 1) * 128] = null[j : j + 1, :]
+        below = jnp.concatenate([caps[...], jnp.zeros((8, D), f32)], axis=0).astype(bf16)
+        for i in range(NR):
+            noisy[i, ROWS:BLK, :] = below
+
+        @pl.loop(0, NR)
+        def _(i):
+            token = (
+                lax.broadcasted_iota(jnp.int32, (ROWS, 128), 0) + (scalars[0, 2] + i * ROWS)
+            ).astype(f32)
+            frame = jnp.floor((token + 0.5) * (1.0 / (GRID_H * GRID_W)))
+            rest = token - frame * (GRID_H * GRID_W)
+            row = jnp.floor((rest + 0.5) * (1.0 / GRID_W))
+            column = rest - row * GRID_W
+            lane = lax.broadcasted_iota(jnp.int32, (ROWS, 128), 1).astype(f32)
+            place = jnp.where(
+                lane < 32.0, frame, jnp.where(lane < 64.0, row + 32.0, column + 64.0)
+            )
+            both = jnp.dot(
+                jnp.where(lane == place, 1.0, 0.0), table[...],
+                preferred_element_type=f32, precision=lax.Precision.HIGHEST,
+            )
+            rows = pl.ds(pl.multiple_of(i * ROWS, ROWS), ROWS)
+            cos[rows, :] = both[:, 0:128]
+            sin[rows, :] = both[:, 128:256]
+
+        def scale_w(gain, lo, hi):
+            @pl.loop(0, 5)
+            def _(t):
+                columns = gain[pl.ds(pl.multiple_of(t * 8, 8), 8), :].T
+                for n in range(8):
+                    rows = pl.ds(pl.multiple_of(t * 1024 + n * 128, 128), 128)
+                    wall[rows, lo:hi] = (
+                        wall[rows, lo:hi].astype(f32) * columns[:, n : n + 1]
+                    ).astype(bf16)
+
         for c in w_copies[:4]:
             c.wait()
+        scale_w(cgain, 0, 384)
+        scale_w(tgain, 384, 512)
 
         @pl.loop(0, NR)
         def _(i):
@@ -245,8 +275,6 @@
                 )
 
         weights_2(wcx, WC2)
-        cos_copy.wait()
-        sin_copy.wait()
 
         def attention(col, row, scale_ref, gains, tables, keep, out):
             q_ref, k_ref, v_ref = tables
@@ -288,21 +316,28 @@
                 out(rows, dot(prob, v_ref[...]).astype(bf16))
 
         def to_a(rows, x):
-            att_a[rows, :] = x
+            gt[rows, :] = x
 
         def to_fake(rows, x):
             fa[rows, :] = x
 
         def to_guided(rows, x):
             gt[rows, :] = (
-                guidance * att_a[rows, :].astype(f32) - (guidance - 1.0) * x.astype(f32)
+                guidance * gt[rows, :].astype(f32) - (guidance - 1.0) * x.astype(f32)
             ).astype(bf16)
 
         attention(0, 0, rc, cqk, (qr, kr, vv), True, to_fake)
         tokens(fa, ac, EA)
+
+        for n in range(2):
+            other = pl.ds(pl.multiple_of((n * 2 + 1 - core) * ROWS, ROWS), ROWS)
+            send(fa.at[other, :], pair.at[n, :, pl.ds(HEAD, HEAD)], FX, sibling)
+            own = pl.ds(pl.multiple_of((n * 2 + core) * ROWS, ROWS), ROWS)
+            pair[n, :, 0:HEAD] = fa[own, :]
         weights_2(wtx, WT2)
         for c in w_copies[4:]:
             c.wait()
+        scale_w(tgain, 512, 768)
 
         @pl.loop(0, NR)
         def _(i):
@@ -319,13 +354,15 @@
         pltpu.VMEM((LEN, HEAD), bf16),
         pltpu.VMEM((LEN, HEAD), bf16),
         pltpu.VMEM((LEN, HEAD), bf16),
-        pltpu.VMEM((LEN, HEAD), bf16),
     )
 
-    noise = level[0:1, 0:1]
-
-    def later_phase(cout, diff_out, fake, abs_out, qgout, qgown, gk, gv, rgt, og8, ogown):
-        cout_copy = local(cout_h, cout, lsem.at[16])
+    fraction = (jnp.full((1, 128), scalars[0, 1], jnp.int32).astype(f32) + 1.0) / 1001.0
+    noise = (5.0 * fraction / (1.0 + 4.0 * fraction))[:, 0:1]
+
+    def later_phase(
+        gaout, diff_out, fake, abs_out, qgopp, qgdir, qgkeep, qgsum, qgown, gk, gv, rgt,
+        ogown, ogout,
+    ):
         tile_cols = pl.ds(pl.multiple_of(myc * COLS, COLS), COLS)
         weights_3(wcx, WC3)
         wait_in(gen, EG)
@@ -350,30 +387,41 @@
             rows = pl.ds(i * 128, 128)
             fake_pred = predictions(i, product(ac, wcx, rows), False)
             target = gen[rows, :].astype(f32)
-            cotf[me, rows, :] = (-noise * (fake_pred - target) * (1.0 / 64.0)).astype(bf16)
+            cotf[z_hi * 8 + s, rows, :] = (-noise * (fake_pred - target) * (1.0 / 64.0)).astype(bf16)
             fake[rows, :] = fake_pred
 
+        cotangent(0)
+        cotangent(1)
+
+        @pl.loop(0, 8)
+        def _(j):
+            four = wcx[pl.ds(j * 4, 4)].reshape(4 * HEAD, COLS)
+            part = dot_nt(cotf[z_hi * 8 + s], four)
+            for m in range(4):
+                gaout[j * 4 + m] = part[:, m * HEAD : (m + 1) * HEAD].astype(bf16)
+
+        @pl.loop(1, NB)
+        def _(k):
+            q = peer(k)
+            send(gaout.at[q], gain_in.at[me], EB, plane(q))
+
+        local_in(gaout.at[me], gain_in.at[me], EB)
+
         top, low = pl.ds(0, 128), pl.ds(128, 128)
-        cotangent(0)
+        chip = z_hi * 8 + s
         for k in (2, 1, 3):
-            send(cotf.at[me, top, :], cotf.at[me, top, :], C1A, along_x(k))
-        cotangent(1)
-        for k in (2, 1, 3):
-            send(cotf.at[me, low, :], cotf.at[me, low, :], C1B, along_z(k))
+            send(cotf.at[chip, top, :], cotf.at[chip, top, :], C1A, along_x(k))
+            send(cotf.at[chip, low, :], cotf.at[chip, low, :], C1B, along_z(k))
         wait_in(cotf.at[pl.ds(0, 3), top, :], C1A)
-        x_run = pl.ds(me - x_at, 4)
+        x_run = pl.ds(chip - x_at, 4)
         for k in (2, 1, 3):
             send(cotf.at[x_run, top, :], cotf.at[x_run, top, :], C2A, along_z(k))
         wait_in(cotf.at[pl.ds(0, 3), low, :], C1B)
         for k in (2, 1, 3):
             for z in range(4):
-                held = cotf.at[(z // 2) * 16 + core * 8 + (z % 2) * 4 + x_at, low, :]
+                held = cotf.at[z * 4 + x_at, low, :]
                 send(held, held, C2B, along_x(k))
-        cout_copy.wait()
-        wait_in(cotf.at[pl.ds(0, 12), top, :], C2A)
-        wait_in(cotf.at[pl.ds(0, 12), low, :], C2B)
-        for run in runs:
-            send(cotf.at[run], cotf.at[run], C3, sibling)
+        wait_in(gain_in, EB)
 
         gk[...] = jnp.zeros_like(gk)
         gv[...] = jnp.zeros_like(gv)
@@ -388,50 +436,23 @@
             )
             return back.astype(bf16).astype(f32)
 
-        def backward_rows(side):
-            @pl.loop(0, 2)
-            def _(j):
-                i = j * 2 + side
-                rows = pl.ds(pl.multiple_of(i * ROWS, ROWS), ROWS)
-                total = jnp.zeros((ROWS, HEAD), f32)
-                for c in range(8):
-                    total += dot_nt(cotf[tile_of(i, c)], cout[:, c * COLS : (c + 1) * COLS])
-                grads = total.astype(bf16)
-                inverse = linv[rows, :][:, 0:1]
-                prob = jnp.exp(dot_nt(qr[rows, :], kr[...]) * score_scale) * inverse
-                grad_prob = dot_nt(grads, vv[...])
-                mean = jnp.sum(grad_prob * prob, axis=1, keepdims=True)
-                grad_score = (prob * (grad_prob - mean) * score_scale).astype(bf16)
-                gq = dot(grad_score, kr[...])
-                gk[...] += dot_tn(qr[rows, :], grad_score)
-                gv[...] += dot_tn(grads, prob.astype(bf16))
-                rg = rc[i] * undo(rows, qraw, invq, cqk[0:1, :], gq)
-                rgt[0:HEAD, rows] = rg.T.astype(bf16)
-
-        backward_rows(core)
-        wait_in(cotf.at[pl.ds(0, 16)], C3)
-
-        def og_share(target, put):
-            for half in range(2):
-                total = jnp.zeros((HEAD, COLS), f32)
-                for r in range(NR):
-                    total += dot_tn(
-                        fa[r * ROWS : (r + 1) * ROWS, :], cotf[tile_of(r, target * 2 + half)]
-                    )
-                put(pl.ds(half * COLS, COLS), total)
-
-        @pl.loop(0, 3)
-        def _(n):
-            off = lax.rem(n + 1, 3) + 1
-            target = lax.rem(w + off, 4)
-
-            def put8(cols, x):
-                og8[off - 1, :, cols] = x.astype(bf16)
-
-            og_share(target, put8)
-            send(og8.at[off - 1], og8in.at[off - 1], E8, {"rep": target})
-
-        backward_rows(1 - core)
+        @pl.loop(0, NR)
+        def _(i):
+            rows = pl.ds(pl.multiple_of(i * ROWS, ROWS), ROWS)
+            total = jnp.zeros((ROWS, HEAD), f32)
+            for c in range(8):
+                total += gain_in[tile_of(i, c)].astype(f32)
+            grads = total.astype(bf16)
+            inverse = linv[rows, :][:, 0:1]
+            prob = jnp.exp(dot_nt(qr[rows, :], kr[...]) * score_scale) * inverse
+            grad_prob = dot_nt(grads, vv[...])
+            mean = jnp.sum(grad_prob * prob, axis=1, keepdims=True)
+            grad_score = (prob * (grad_prob - mean) * score_scale).astype(bf16)
+            gq = dot(grad_score, kr[...])
+            gk[...] += dot_tn(qr[rows, :], grad_score)
+            gv[...] += dot_tn(grads, prob.astype(bf16))
+            rg = rc[i] * undo(rows, qraw, invq, cqk[0:1, :], gq)
+            rgt[0:HEAD, rows] = rg.T.astype(bf16)
 
         for i in range(NR):
             rows = pl.ds(i * ROWS, ROWS)
@@ -450,21 +471,42 @@
                 total = row_sum * caps[0:1, cols]
                 for i in range(NR):
                     total += dot(rgt[:, i * ROWS : (i + 1) * ROWS], noisy[i, 0:ROWS, cols])
-                put(pl.ds(pl.multiple_of(j * 256, 256), 256), total * cgain[0:1, cols])
-
-        for off in (2, 1, 3):
-            target = lax.rem(w + off, 4)
-
-            def put(cols, x, off=off):
-                qgout[off - 1, :, cols] = x.astype(bf16)
-
-            share(target, put)
-            send(qgout.at[off - 1], qgin.at[off - 1], EQ, {"rep": target})
+                lines = cgain[pl.ds(target * (FEAT // 128) + j * 2, 2), :]
+                gains = jnp.concatenate([lines[0:1], lines[1:2]], axis=1)
+                put(pl.ds(pl.multiple_of(j * 256, 256), 256), total * gains)
+
+        first, second = pl.ds(0, 192), pl.ds(192, 192)
+        up, down = window(1), window(3)
+
+        def put_opposite(cols, x):
+            qgopp[0, :, cols] = x[0:192].astype(bf16)
+            qgopp[1, :, cols] = x[192:384].astype(bf16)
+
+        def put_up(cols, x):
+            qgkeep[0, :, cols] = x[0:192]
+            qgdir[0, :, cols] = x[192:384].astype(bf16)
+
+        def put_down(cols, x):
+            qgdir[1, :, cols] = x[0:192].astype(bf16)
+            qgkeep[1, :, cols] = x[192:384]
 
         def put_own(cols, x):
             qgown[:, cols] = x
 
+        share(lax.rem(w + 2, 4), put_opposite)
+        send(qgopp.at[0], qgfwd.at[0], QF0, up)
+        send(qgopp.at[1], qgfwd.at[1], QF1, down)
+        share(lax.rem(w + 1, 4), put_up)
+        send(qgdir.at[0], qgin.at[0, second, :], QD0, up)
+        share(lax.rem(w + 3, 4), put_down)
+        send(qgdir.at[1], qgin.at[1, first, :], QD1, down)
         share(w, put_own)
+        wait_in(qgfwd.at[0], QF0)
+        qgsum[0] = (qgkeep[0] + qgfwd[0].astype(f32)).astype(bf16)
+        send(qgsum.at[0], qgin.at[0, first, :], QC0, up)
+        wait_in(qgfwd.at[1], QF1)
+        qgsum[1] = (qgkeep[1] + qgfwd[1].astype(f32)).astype(bf16)
+        send(qgsum.at[1], qgin.at[1, second, :], QC1, down)
 
         weights_3(wtx, WT3)
         wait_in(ag, EU)
@@ -510,7 +552,33 @@
             def _():
                 send(src, diff_mine, ED, {"branch": to_b, "seq": to_s})
 
-        og_share(w, lambda cols, x: ogown.__setitem__((slice(None), cols), x))
+        wait_in(pair.at[:, :, pl.ds(0, HEAD)], FX)
+        wait_in(cotf.at[pl.ds(0, 12), top, :], C2A)
+        wait_in(cotf.at[pl.ds(0, 12), low, :], C2B)
+
+        @pl.loop(0, 8)
+        def _(c):
+            base = (c // 4) * 8 + lax.rem(c, 4)
+            total = dot_tn(pair[0], cotf[base]) + dot_tn(pair[1], cotf[base + 4])
+            cols = pl.ds(pl.multiple_of(c * COLS, COLS), COLS)
+            ogown[:, cols] = total[0:HEAD]
+            ogout[:, cols] = total[HEAD:].astype(bf16)
+
+        send(ogout, ogsib, CS, sibling)
+        wait_in(ogsib, CS)
+        wait_out(ogsib, CS)
+
+        @pl.loop(0, 4)
+        def _(n):
+            cols = pl.ds(pl.multiple_of(n * FEAT, FEAT), FEAT)
+            total = ogown[:, cols] + ogsib[:, cols].astype(f32)
+            ogown[:, cols] = total
+            ogout[:, cols] = total.astype(bf16)
+
+        for off in (2, 1, 3):
+            target = lax.rem(w + off, 4)
+            shared = pl.ds(pl.multiple_of(target * FEAT, FEAT), FEAT)
+            send(ogout.at[:, shared], og8in.at[off - 1], E8, {"rep": target})
 
         wait_in(abs_in, ES)
         wait_in(diff_in, ED)
@@ -526,29 +594,37 @@
 
         gg_copy = local(diff_in, gg_h, lsem.at[17])
 
-        wait_in(og8in, E8)
-        for j in range(5):
-            cols = slice(j * 256, (j + 1) * 256)
-            total = ogown[:, cols]
-            for off in range(3):
-                total += og8in[off, :, cols].astype(f32)
-            ogown[:, cols] = total
-        og_copy = local(ogown, og_h, lsem.at[19])
-        wait_in(qgin, EQ)
+        wait_in(qgin.at[0, second, :], QD0)
+        wait_in(qgin.at[1, first, :], QD1)
+        wait_in(qgin.at[0, first, :], QC0)
+        wait_in(qgin.at[1, second, :], QC1)
 
         def sum_q(out):
+            copies = []
             for m in range(3):
+                if m == 2:
+                    copies[0].wait()
                 for j in range(FEAT // 256):
                     rows = slice(m * HEAD, (m + 1) * HEAD)
                     cols = slice(j * 256, (j + 1) * 256)
                     total = qgown[rows, cols]
-                    for off in range(3):
-                        total += qgin[off, rows, cols].astype(f32)
-                    out[m, j * 256 : (j + 1) * 256, :] = total.T
-            local(out, qg_h, lsem.at[18]).wait()
-
-        pl.run_scoped(sum_q, pltpu.VMEM((3, FEAT, HEAD), f32))
-        og_copy.wait()
+                    for way in range(2):
+                        total += qgin[way, rows, cols].astype(f32)
+                    out[m % 2, j * 256 : (j + 1) * 256, :] = total.T
+                copies.append(local(out.at[m % 2], qg_h.at[m], lsem.at[4 + m]))
+            copies[1].wait()
+            copies[2].wait()
+
+        pl.run_scoped(sum_q, pltpu.VMEM((2, FEAT, HEAD), f32))
+        wait_in(og8in, E8)
+        ogsum = ogown.at[:, pl.ds(pl.multiple_of(w * FEAT, FEAT), FEAT)]
+        for j in range(5):
+            cols = slice(j * 256, (j + 1) * 256)
+            total = ogsum[:, cols]
+            for off in range(3):
+                total += og8in[off, :, cols].astype(f32)
+            ogsum[:, cols] = total
+        local(ogsum, og_h, lsem.at[19]).wait()
         gg_copy.wait()
 
         for dst, e in ((wcx, WC1), (wtx, WT1)):
@@ -566,7 +642,8 @@
         wait_out(cotf.at[pl.ds(0, 3), low, :], C1B)
         wait_out(cotf.at[pl.ds(0, 12), top, :], C2A)
         wait_out(cotf.at[pl.ds(0, 12), low, :], C2B)
-        wait_out(cotf.at[pl.ds(0, 16)], C3)
+        wait_out(pair.at[:, :, pl.ds(0, HEAD)], FX)
+        wait_out(gain_in.at[pl.ds(0, NB - 1)], EB)
         wait_out(abs_in.at[pl.ds(0, NB - 1)], ES)
 
         @pl.when(has_rows)
@@ -577,22 +654,26 @@
         def _():
             wait_out(diff_in, ED)
 
-        wait_out(qgin, EQ)
+        for way, e in ((0, QF0), (1, QF1), (0, QD0), (1, QD1), (0, QC0), (1, QC1)):
+            wait_out(qgfwd.at[way], e)
         wait_out(og8in, E8)
 
     pl.run_scoped(
         later_phase,
-        pltpu.VMEM((HEAD, D), bf16),
+        pltpu.VMEM((NB, ROWS, HEAD), bf16),
         pltpu.VMEM((ROWS, COLS), bf16),
         pltpu.VMEM((ROWS, COLS), f32),
         pltpu.VMEM((8, 128), f32),
-        pltpu.VMEM((3, 3 * HEAD, FEAT), bf16),
+        pltpu.VMEM((2, 192, FEAT), bf16),
+        pltpu.VMEM((2, 192, FEAT), bf16),
+        pltpu.VMEM((2, 192, FEAT), f32),
+        pltpu.VMEM((2, 192, FEAT), bf16),
         pltpu.VMEM((3 * HEAD, FEAT), f32),
         pltpu.VMEM((HEAD, LEN), f32),
         pltpu.VMEM((HEAD, LEN), f32),
         pltpu.VMEM((3 * HEAD, LEN), bf16),
-        pltpu.VMEM((3, HEAD, FEAT), bf16),
-        pltpu.VMEM((HEAD, FEAT), f32),
+        pltpu.VMEM((HEAD, D), f32),
+        pltpu.VMEM((HEAD, D), bf16),
     )
 
 
@@ -601,15 +682,7 @@
     teacher_qkv, teacher_out, teacher_gain, teacher_qk_gain,
     critic_qkv, critic_out, critic_gain, critic_qk_gain,
 ):
-    fraction = (timestep.astype(f32) + 1.0) / 1001.0
-    noise_level = 5.0 * fraction / (1.0 + 4.0 * fraction)
-    used_caption = jnp.where(caption_drop[0] == 1, null_caption, caption[0])
-    caps16 = jnp.zeros((PAD, D), bf16).at[0].set(used_caption).at[1].set(null_caption)
-    caps = jnp.concatenate([caps16[0:8].astype(f32)], axis=0)
-    cosine, sine = rope_tables(window_start[0])
-    wc = (critic_qkv.astype(f32) * critic_gain[None, :, None]).astype(bf16)
-    wt = (teacher_qkv.astype(f32) * teacher_gain[None, :, None]).astype(bf16)
-    level = jnp.broadcast_to(noise_level[:, None], (8, 128))
+    scalars = jnp.stack([caption_drop, timestep, window_start], axis=1)
     hbm = pl.BlockSpec(memory_space=pl.ANY)
     vmem = pl.BlockSpec(memory_space=pltpu.VMEM)
     gg, qg, og = pl.pallas_call(
@@ -620,7 +693,7 @@
             jax.ShapeDtypeStruct((3, FEAT, HEAD), f32),
             jax.ShapeDtypeStruct((HEAD, FEAT), f32),
         ),
-        in_specs=[hbm] * 6 + [vmem] * 5 + [hbm] * 3,
+        in_specs=[pl.BlockSpec(memory_space=pltpu.SMEM)] + [hbm] * 3 + [vmem] * 7 + [hbm] * 3,
         out_specs=(hbm, hbm, hbm),
         scratch_shapes=[
             pltpu.VMEM((NR, BLK, D), bf16),
@@ -628,14 +701,19 @@
             pltpu.VMEM((NB, HEAD, COLS), bf16),
             pltpu.VMEM((ROWS, NB * HEAD), bf16),
             pltpu.VMEM((ROWS, NB * HEAD), bf16),
-            pltpu.VMEM((NB, ROWS, COLS), bf16),
-            pltpu.VMEM((3, 3 * HEAD, FEAT), bf16),
+            pltpu.VMEM((NB, ROWS, HEAD), bf16),
+            pltpu.VMEM((NB // 2, ROWS, COLS), bf16),
+            pltpu.VMEM((2, ROWS, 2 * HEAD), bf16),
+            pltpu.VMEM((HEAD, D), bf16),
+            pltpu.VMEM((2, 3 * HEAD, FEAT), bf16),
+            pltpu.VMEM((2, 192, FEAT), bf16),
             pltpu.VMEM((3, HEAD, FEAT), bf16),
             pltpu.VMEM((128, D), bf16),
             pltpu.VMEM((NB, 8, 128), f32),
             pltpu.VMEM((ROWS, COLS), bf16),
             pltpu.VMEM((LEN, HEAD), f32),
             pltpu.VMEM((LEN, HEAD), f32),
+            pltpu.VMEM((8, D), f32),
             pltpu.VMEM((LEN, HEAD), f32),
             pltpu.VMEM((LEN, HEAD), f32),
             pltpu.VMEM((LEN, HEAD), bf16),
@@ -649,15 +727,18 @@
             pltpu.VMEM((LEN, HEAD), bf16),
             pltpu.VMEM((LEN, HEAD), bf16),
             pltpu.SemaphoreType.DMA((20,)),
-            pltpu.SemaphoreType.DMA((18,)),
-            pltpu.SemaphoreType.DMA((18,)),
+            pltpu.SemaphoreType.DMA((25,)),
+            pltpu.SemaphoreType.DMA((25,)),
         ],
         compiler_params=pltpu.CompilerParams(
-            collective_id=0, has_side_effects=True, vmem_limit_bytes=64 * 1024 * 1024
+            collective_id=0, has_side_effects=True, vmem_limit_bytes=127 * 512 * 1024
         ),
     )(
-        noisy[0], wc, wt, caps16, cosine, sine, critic_qk_gain, teacher_qk_gain, level, caps,
-        critic_gain[None, :], generated[0], critic_out, teacher_out,
+        scalars, noisy[0], critic_qkv, teacher_qkv,
+        caption.reshape(40, 128).astype(f32), null_caption.reshape(40, 128).astype(f32),
+        rope_table(), critic_qk_gain, teacher_qk_gain,
+        critic_gain.reshape(40, 128), teacher_gain.reshape(40, 128),
+        generated[0], critic_out, teacher_out,
     )
     return (gg[None], qg, og)
 

time: 212 us -> 186 us (0.88); the launches traced: 212 us -> 182 us
  Pallas kernels: 187 us -> 170 us
  other arithmetic: 15.7 us -> 4.42 us
    pallas_call x1, Pallas kernels: 187 us -> 170 us  [body(): pl.pallas_call(step_kernel, name='generator_step', out_shape=(jax.ShapeDt...]
    convert_element_type x2, other arithmetic: 7.62 us -> 2.67 us  [the longest x1 1.36 us: body(): caption.reshape(40, 128).astype(f32)]
    neg x1 -> x0, other arithmetic: 4.52 us -> none  [rope_tables(): -sine]
    unnamed x15 -> x7, local copies, waits for them, and re-layouts: 4.75 us -> 4.97 us
where the time goes in v3:
time: 186 us; the launch traced here: 182 us
  Pallas kernels  170 us (91%)
  local copies, waits for them, and re-layouts  4.97 us (3%)
  other arithmetic  4.42 us (2%)
  between operations  2.61 us (1%)
    pallas_call x1, Pallas kernels, body(): pl.pallas_call(step_kernel, name='generator_step', out_shape=(jax.ShapeDt...  170 us
    unnamed x7, local copies, waits for them, and re-layouts  4.97 us

profile of v3, /device:TPU:1, one launch (start us, length us, event | category | flops | bytes accessed | tf_op | source)
XLA Modules:
  0.0 182.5 jit_solution(13693763387516062742)
XLA Ops:
  2.6 0.6 pad_add_fusion.scalars
  3.2 1.4 convert_element_type.44
  4.6 1.3 bitcast_convert_fusion.null_caption
  5.9 0.3 compare_select_fusion.1
  6.2 0.8 pad_maximum_fusion.table
  7.0 170.4 %generator_step.1 = (bf16[128,5120]{1,0:T(8,128)(2,1)}, f32[3,1280,128]{2,1,0:T(8,128)}, f32[128,1280]{1,0:T(8,128)}) custom-call(s32[1,3]{1,0:T(1,128)} %pad_add_fusion.scalars, bf16[1024,5120]{1,0:T(8,128)(2,1)} %bitcast.15, bf16[3,5120,128]{2,1,0:T(8,128)(2,1)} %wc_h.1, bf16[3,5120,128]{2,1,0:T(8,128)(2,1)} %wt_h.1, f32[40,128]{1,0:T(8,128)} %bitcast.18, ...), custom_call_target="tpu_custom_call" | custom-call | tf_op jit(solution)/shard_map/generator_step/pallas_call | solution.py:688
  177.5 0.0 copy-start
  177.5 2.6 %copy.24 = bf16[1,128,5120]{2,1,0:T(8,128)(2,1)} copy(bf16[1,128,5120]{2,1,0:T(8,128)(2,1)} %bitcast.17) | data formatting | bytes 2621440
  180.1 0.0 copy-done
  180.1 0.0 copy-start.1
  180.1 1.3 copy.25
  181.4 0.3 copy-done.1
  181.6 0.8 copy.26
  (3 shorter events, 0.0 us)
Async XLA Ops:
  177.5 2.6 %copy-start = (f32[3,1280,128]{2,1,0:T(8,128)S(1)}, f32[3,1280,128]{2,1,0:T(8,128)}, u32[]{:S(2)}) copy-start(f32[3,1280,128]{2,1,0:T(8,128)} %get-tuple-element.18) | copy-start | bytes 5898244
  180.1 1.5 copy-start.1
